TPU v7x, 32 devices: a whole 2x2x4 slice. The times are simulated.
32 devices in a mesh: grp: 2 (over y), ctx: 16 (over z, x, core).
Axes of the slice: x: 2, y: 2, z: 4, core: 2. Of those that a mesh axis runs over, the one named last changes fastest.
Arguments:
- query_main: bfloat16 [64, 128, 576], P(('grp', 'ctx')), parts along dimension 0, may hold values from -3 to 3
- key_codes: bfloat16 [4096, 576], P(('grp', 'ctx')), parts along dimension 0, may hold values from -4 to 4
- key_scales: int32 [4096, 4], P(('grp', 'ctx')), parts along dimension 0, may hold values from -2 to 2
- index_keys: bfloat16 [4096, 128], P(('grp', 'ctx')), parts along dimension 0, may hold values from -5 to 5
- index_query: bfloat16 [64, 64, 128], P(('grp', 'ctx')), parts along dimension 0, may hold values from -7 to 7
- index_weight: float32 [64, 64], P(('grp', 'ctx')), parts along dimension 0, may hold values from -4 to 4
- query_pos: int32 [64], P(('grp', 'ctx')), parts along dimension 0, may hold values from 1024 to 2047
Outputs:
- grad_index_query: float32 [64, 64, 128], P(('grp', 'ctx')), parts along dimension 0
- grad_index_weight: float32 [64, 64], P(('grp', 'ctx')), parts along dimension 0
- grad_index_keys: float32 [4096, 128], P(('grp', 'ctx')), parts along dimension 0
There are 2 independent parts, one for each index of `grp`. A program takes and returns all parts, laid end to end along the dimension named above; each array names one. Nothing has to cross between parts.
All inputs are finite; a program needn't handle non-finite values.
Results may differ from a plain program's by a relative error of at most 0.005.
Values may be sent and summed in bfloat16 or wider, within the bound.
No kernel may reach another device: no remote copies, remote signals or barrier semaphores. Data moves between devices by JAX's collectives and lax.ppermute only.
A program may use at most 192 MiB of HBM per device.

v0:
```python
import math

import jax
import jax.numpy as jnp
from jax import lax
from jax.sharding import PartitionSpec as P

ROPE = 64


main_scale = 192.0 ** (-0.5)


def dot_rows(left, right):
    return lax.dot_general(
        left, right, (((1,), (1,)), ((), ())), preferred_element_type=jnp.float32
    )


def dequantize(key_codes, factors):
    key_count = key_codes.shape[0]
    groups = factors.shape[1]
    group_width = (key_codes.shape[1] - ROPE) // groups
    scaled = (
        key_codes[:, : groups * group_width]
        .astype(jnp.float32)
        .reshape(key_count, groups, group_width)
    )
    scaled = scaled * factors.astype(jnp.float32)[:, :, None]
    rotary = key_codes[:, groups * group_width :].astype(jnp.float32)
    return jnp.concatenate([scaled.reshape(key_count, -1), rotary], axis=1).astype(jnp.bfloat16)


def sweep_blocks(visit, running, arrays):
    key_count = arrays[0].shape[0]
    block_rows = math.gcd(key_count, 512)

    def visit_block(block, state):
        lower = block * block_rows
        rows = tuple((lax.dynamic_slice_in_dim(array, lower, block_rows, 0) for array in arrays))
        return visit(state, rows, lower)

    return lax.fori_loop(0, key_count // block_rows, visit_block, running)


def body(query_main, key_codes, key_scales, index_keys, index_query, index_weight, query_pos):
    query_rows, head_count, latent_width = query_main.shape
    index_heads = index_query.shape[1]
    index_width = index_query.shape[2]
    main_flat = query_main.reshape(query_rows * head_count, latent_width)
    query_flat = index_query.reshape(query_rows * index_heads, index_width)
    own_keys = key_codes.shape[0]
    key_total = own_keys * lax.axis_size("ctx")
    index_scale = float(index_heads * index_width) ** (-0.5)
    factors = jnp.exp2(key_scales.astype(jnp.float32)).astype(jnp.bfloat16)
    gathered_query = lax.all_gather(index_query, "ctx", axis=0, tiled=True)
    gathered_weight = lax.all_gather(index_weight, "ctx", axis=0, tiled=True)

    def index_part(key_rows, first_key):
        row_count = key_rows.shape[0]
        key_pos = first_key + lax.iota(jnp.int32, row_count)
        visible = key_pos[None, :] <= query_pos[:, None]
        head_dots = dot_rows(query_flat, key_rows).reshape(query_rows, index_heads, row_count)
        index_score = index_scale * jnp.sum(
            index_weight[:, :, None] * jnp.maximum(head_dots, 0.0), axis=1
        )
        index_exp = jnp.where(visible, jnp.exp(index_score), 0.0)
        return (index_exp, head_dots, visible)

    def add_norms(running, rows, first_key):
        latent_rows, key_rows = rows
        main_sum, index_sum, main_store = running
        row_count = latent_rows.shape[0]
        index_exp, head_dots, visible = index_part(key_rows, first_key)
        main_score = (
            dot_rows(main_flat, latent_rows).reshape(query_rows, head_count, row_count) * main_scale
        )
        main_exp = jnp.where(visible[:, None, :], jnp.exp(main_score), 0.0)
        main_store = lax.dynamic_update_slice_in_dim(main_store, main_exp, first_key, 2)
        return (
            main_sum + jnp.sum(main_exp, axis=2),
            index_sum + jnp.sum(index_exp, axis=1),
            main_store,
        )

    empty_norms = (
        jnp.zeros((query_rows, head_count), jnp.float32),
        jnp.zeros((query_rows,), jnp.float32),
        jnp.zeros((query_rows, head_count, key_total), jnp.float32),
    )
    empty_buffer = jnp.zeros((query_rows, key_total), jnp.float32)
    empty_terms = (
        jnp.zeros((query_rows, index_heads), jnp.float32),
        jnp.zeros((query_rows * index_heads, index_width), jnp.float32),
        empty_buffer,
    )

    def make_terms(main_total, index_total, main_store):

        def add_terms(running, rows, first_key):
            key_rows = rows[0]
            row_count = key_rows.shape[0]
            grad_weight, grad_query, buffer = running
            index_exp, head_dots, visible = index_part(key_rows, first_key)
            main_exp = lax.dynamic_slice_in_dim(main_store, first_key, row_count, 2)
            target = jnp.sum(main_exp / main_total[:, :, None], axis=1) / head_count
            index_prob = index_exp / index_total[:, None]
            gradient = key_total * (index_prob - target)
            grad_weight = grad_weight + index_scale * jnp.sum(
                gradient[:, None, :] * jnp.maximum(head_dots, 0.0), axis=2
            )
            grad_dots = jnp.where(
                head_dots > 0, index_scale * gradient[:, None, :] * index_weight[:, :, None], 0.0
            )
            grad_dots = grad_dots.astype(jnp.bfloat16).reshape(query_rows * index_heads, -1)
            grad_query = grad_query + jnp.dot(
                grad_dots, key_rows, preferred_element_type=jnp.float32
            )
            buffer = lax.dynamic_update_slice_in_dim(buffer, gradient, first_key, 1)
            return (grad_weight, grad_query, buffer)

        return add_terms

    codes_all, factors_all, keys_all = (
        lax.all_gather(key_codes, "ctx", axis=0, tiled=True),
        lax.all_gather(factors, "ctx", axis=0, tiled=True),
        lax.all_gather(index_keys, "ctx", axis=0, tiled=True),
    )
    latent = dequantize(codes_all, factors_all)
    norms = sweep_blocks(add_norms, empty_norms, (latent, keys_all))
    main_total, index_total, main_store = norms
    grad_weight, grad_query, buffer = sweep_blocks(
        make_terms(main_total, index_total, main_store), empty_terms, (keys_all,)
    )
    owner_grad = lax.all_to_all(buffer, "ctx", split_axis=1, concat_axis=0, tiled=True)
    all_rows = gathered_query.shape[0]
    all_flat = gathered_query.reshape(all_rows * index_heads, index_width)
    owner_dots = dot_rows(all_flat, index_keys).reshape(all_rows, index_heads, own_keys)
    owner_terms = jnp.where(
        owner_dots > 0, index_scale * owner_grad[:, None, :] * gathered_weight[:, :, None], 0.0
    )
    owner_terms = owner_terms.astype(jnp.bfloat16).reshape(all_rows * index_heads, own_keys)
    key_grad = lax.dot_general(
        owner_terms, all_flat, (((0,), (0,)), ((), ())), preferred_element_type=jnp.float32
    )
    return (grad_query.reshape(query_rows, index_heads, index_width), grad_weight, key_grad)


def solution(mesh):
    placed = (
        P(("grp", "ctx"), None, None),
        P(("grp", "ctx"), None),
        P(("grp", "ctx"), None),
        P(("grp", "ctx"), None),
        P(("grp", "ctx"), None, None),
        P(("grp", "ctx"), None),
        P(("grp", "ctx")),
    )
    return jax.shard_map(
        body,
        mesh=mesh,
        in_specs=placed,
        out_specs=(P(("grp", "ctx"), None, None), P(("grp", "ctx"), None), P(("grp", "ctx"), None)),
        check_vma=False,
    )
```

profile of v0, /device:TPU:0, one launch (start us, length us, event | category | flops | bytes accessed | tf_op | source)
XLA Modules:
  0.0 141.3 jit_solution(3682944358466345611)
XLA Ops:
  7.2 1.7 %copy.17 = bf16[128,576]{1,0:T(8,128)(2,1)} copy(bf16[128,576]{0,1:T(8,128)(2,1)} %param.12) | data formatting | bytes 294912 | tf_op args[1]
  9.0 0.7 exponential_convert_fusion
  9.7 23.1 %all_gather.17 = bf16[2048,4]{0,1:T(4,128)(2,1)S(1)} all-gather(bf16[128,4]{0,1:T(4,128)(2,1)S(1)} %exponential_convert_fusion), channel_id=1, replica_groups=mesh['grp'=2,'ctx'=16] {'ctx'}, dimensions={0}, use_global_device_ids=true | all-gather | bytes 17408 | tf_op jit(solution)/shard_map/all_gather | solution.py:126
  32.8 0.3 copy.18
  33.1 1.2 copy.19
  34.2 0.8 mul.336
  35.0 20.3 %all_gather.15 = bf16[2048,128]{1,0:T(8,128)(2,1)S(1)} all-gather(bf16[128,128]{1,0:T(8,128)(2,1)} %param.14), channel_id=1, replica_groups=mesh['grp'=2,'ctx'=16] {'ctx'}, dimensions={0}, use_global_device_ids=true | all-gather | bytes 557056 | tf_op jit(solution)/shard_map/all_gather | solution.py:127
  55.2 21.7 %all_gather.18 = bf16[32,64,128]{2,1,0:T(8,128)(2,1)} all-gather(bf16[2,64,128]{2,1,0:T(8,128)(2,1)S(1)} %copy-done), channel_id=1, replica_groups=mesh['grp'=2,'ctx'=16] {'ctx'}, dimensions={0}, use_global_device_ids=true | all-gather | bytes 557056 | tf_op jit(solution)/shard_map/all_gather | solution.py:56
  77.0 4.6 %mul.262 = f32[2048,4,128]{2,1,0:T(4,128)S(1)} broadcast(f32[2048,4]{1,0:T(8,128)S(1)} %copy.18), dimensions={0,1} | broadcast | bytes 4227072 | tf_op jit(solution)/shard_map/mul | solution.py:29
  81.6 0.8 fusion.16
  82.4 0.2 slice-done
  82.7 0.2 pad_maximum_fusion
  82.9 1.6 %broadcast_in_dim.106 = f32[2,128,2048]{2,1,0:T(8,128)} broadcast(f32[]{:T(128)} %constant.144.clone.1), dimensions={} | broadcast | bytes 2097156 | tf_op jit(solution)/shard_map/broadcast_in_dim | solution.py:89
  84.5 7.3 %while.39 = (s32[]{:T(128)}, f32[2,128]{1,0:T(2,128)S(1)}, f32[2]{0:T(128)S(1)}, f32[2,128,2048]{2,1,0:T(8,128)}, s32[2]{0:T(128)S(1)}, /*index=5*/bf16[2048,576...) while((s32[]{:T(128)}, f32[2,128]{1,0:T(2,128)S(1)}, ...), condition=%wide.region_4.5_spmd.clone, body=%wide.region_0.4_spmd.clone.sunk | while | flops 168496896 | bytes 2741494 | solution.py:43
  84.5 0.2 multiply_reduce_fusion.5
  84.9 0.5 fusion.51
  85.4 0.9 select_dynamic-update-slice_fusion.2
  86.4 0.2 multiply_reduce_fusion.5
  86.8 0.5 fusion.51
  87.3 0.9 select_dynamic-update-slice_fusion.2
  88.2 0.2 multiply_reduce_fusion.5
  88.7 0.5 fusion.51
  89.2 0.9 select_dynamic-update-slice_fusion.2
  90.1 0.2 multiply_reduce_fusion.5
  90.5 0.5 fusion.51
  91.0 0.9 select_dynamic-update-slice_fusion.2
  91.9 0.6 broadcast_in_dim.104
  92.5 15.1 %while.40 = (s32[]{:T(128)}, f32[2,64]{1,0:T(2,128)S(1)}, f32[128,128]{1,0:T(8,128)}, f32[2,2048]{1,0:T(2,128)}, s32[2]{0:T(128)S(1)}, /*index=5*/f32[2,64]{1,0:...) while((s32[]{:T(128)}, f32[2,64]{1,0:T(2,128)S(1)}, ...), condition=%wide.wide.region_9.10_spmd.clone, body=%wide.wide.region_5.9_spmd.clone.sunk | while | flops 34512644 | bytes 1792754 | solution.py:43
  92.5 0.2 multiply_reduce_fusion.6
  92.7 1.2 fusion.56
  93.9 0.7 constant_dynamic-update-slice_fusion.3
  94.7 0.8 convolution_add_fusion.3
  95.6 0.2 multiply_reduce_fusion.6
  95.8 1.2 fusion.56
  97.0 0.7 constant_dynamic-update-slice_fusion.3
  97.8 1.7 %convolution_add_fusion.3 = f32[128,128]{1,0:T(8,128)} fusion(bf16[128,512]{1,0:T(8,128)(2,1)S(1)} %get-tuple-element.777, bf16[2048,128]{1,0:T(8,128)(2,1)S(1)} %get-tuple-element.859, s32[]{:T(128)S(6)} %select_n.120, f32[128,128]{1,0:T(8,128)} %get-tuple-element.839, pred[]{:T(512)S(6)} %compare.8), kind=kOutput, calls=%fused_computation.17.clone.clone.1 | convolution fusion | flops 16809984 | bytes 393221 | tf_op jit(solution)/shard_map/while/body/eval_jaxpr/dot_general | solution.py:116
  99.6 0.2 multiply_reduce_fusion.6
  99.8 1.2 fusion.56
  101.0 0.7 constant_dynamic-update-slice_fusion.3
  101.8 1.7 %convolution_add_fusion.3 = f32[128,128]{1,0:T(8,128)} fusion(bf16[128,512]{1,0:T(8,128)(2,1)S(1)} %get-tuple-element.777, bf16[2048,128]{1,0:T(8,128)(2,1)S(1)} %get-tuple-element.859, s32[]{:T(128)S(6)} %select_n.120, f32[128,128]{1,0:T(8,128)} %get-tuple-element.839, pred[]{:T(512)S(6)} %compare.8), kind=kOutput, calls=%fused_computation.17.clone.clone.1 | convolution fusion | flops 16809984 | bytes 393221 | tf_op jit(solution)/shard_map/while/body/eval_jaxpr/dot_general | solution.py:116
  103.6 0.2 multiply_reduce_fusion.6
  103.8 1.2 fusion.56
  105.0 0.7 constant_dynamic-update-slice_fusion.3
  105.8 1.7 %convolution_add_fusion.3 = f32[128,128]{1,0:T(8,128)} fusion(bf16[128,512]{1,0:T(8,128)(2,1)S(1)} %get-tuple-element.777, bf16[2048,128]{1,0:T(8,128)(2,1)S(1)} %get-tuple-element.859, s32[]{:T(128)S(6)} %select_n.120, f32[128,128]{1,0:T(8,128)} %get-tuple-element.839, pred[]{:T(512)S(6)} %compare.8), kind=kOutput, calls=%fused_computation.17.clone.clone.1 | convolution fusion | flops 16809984 | bytes 393221 | tf_op jit(solution)/shard_map/while/body/eval_jaxpr/dot_general | solution.py:116
  107.6 3.5 %all-to-all-start = ((f32[2,16,128]{2,0,1:T(2,128)}), f32[2,16,128]{2,0,1:T(2,128)S(1)}, u32[]{:S(2)}, u32[]{:S(2)}) async-start(f32[2,16,128]{2,0,1:T(2,128)} %bitcast.4), calls=%async_computation | async-start | bytes 32768 | tf_op jit(solution)/shard_map/all_to_all | solution.py:135
  111.1 0.3 fusion.20
  111.4 21.7 %all-gather = f32[16,2,64]{2,1,0:T(2,128)S(1)} all-gather(f32[1,2,64]{2,1,0:T(2,128)S(1)} %bitcast.90), channel_id=1, replica_groups=mesh['grp'=2,'ctx'=16] {'ctx'}, dimensions={0}, use_global_device_ids=true | all-gather | bytes 8704 | tf_op jit(solution)/shard_map/all_gather | solution.py:57
  133.1 1.3 convolution_bitcast_fusion
  (64 shorter events, 1.8 us)
Async XLA Ops:
  7.2 48.1 %copy-start = (bf16[2,64,128]{2,1,0:T(8,128)(2,1)S(1)}, bf16[2,64,128]{2,1,0:T(8,128)(2,1)}, u32[]{:S(2)}) copy-start(bf16[2,64,128]{2,1,0:T(8,128)(2,1)} %param.15) | copy-start | bytes 98308
  7.2 69.8 %all-gather.3.cloned.1.call-start = ((), (), s32[]{:S(2)}) async-start(), calls=%async_computation.1 | async-start | bytes 2785280 | tf_op jit(solution)/shard_map/all_gather | solution.py:125
  77.0 4.7 %copy-start.1 = (bf16[2048,576]{1,0:T(8,128)(2,1)S(1)}, bf16[2048,576]{1,0:T(8,128)(2,1)}, u32[]{:S(2)}) copy-start(bf16[2048,576]{1,0:T(8,128)(2,1)} %all-gather.3.cloned.1.call-done) | copy-start | bytes 7077892
  81.6 1.0 slice-start
  82.7 1.8 %copy-start.3 = (f32[2,64]{1,0:T(2,128)S(1)}, f32[2,64]{1,0:T(2,128)}, u32[]{:S(2)}) copy-start(f32[2,64]{1,0:T(2,128)} %param.16) | copy-start | bytes 1540
  82.7 1.8 %copy-start.4 = (s32[2]{0:T(128)S(1)}, s32[2]{0:T(128)}, u32[]{:S(2)}) copy-start(s32[2]{0:T(128)} %param.17) | copy-start | bytes 28
  92.5 18.6 %copy-start.2 = (bf16[32,64,128]{2,1,0:T(8,128)(2,1)S(1)}, bf16[32,64,128]{2,1,0:T(8,128)(2,1)}, u32[]{:S(2)}) copy-start(bf16[32,64,128]{2,1,0:T(8,128)(2,1)} %all_gather.18) | copy-start | bytes 1572868
  92.5 18.6 %copy-start.5 = (bf16[128,128]{1,0:T(8,128)(2,1)S(1)}, bf16[128,128]{1,0:T(8,128)(2,1)}, u32[]{:S(2)}) copy-start(bf16[128,128]{1,0:T(8,128)(2,1)} %param.14) | copy-start | bytes 98308
  107.6 26.9 %copy-start.6 = (f32[2,64]{1,0:T(2,128)}, f32[2,64]{1,0:T(2,128)S(1)}, u32[]{:S(2)}) copy-start(f32[2,64]{1,0:T(2,128)S(1)} %get-tuple-element.438) | copy-start | bytes 1540
  107.6 25.5 %all-to-all-start = ((f32[2,16,128]{2,0,1:T(2,128)}), f32[2,16,128]{2,0,1:T(2,128)S(1)}, u32[]{:S(2)}, u32[]{:S(2)}) async-start(f32[2,16,128]{2,0,1:T(2,128)} %bitcast.4), calls=%async_computation | async-start | bytes 32768 | tf_op jit(solution)/shard_map/all_to_all | solution.py:135
Sparse Core Ops, SparseCore 0:
  10.3 46.9 all-gather.2
where the time goes:
time: 142 us; the launch traced here: 141 us
  blocking collectives  86.8 us (61%)
  between operations  14.2 us (10%)
  other arithmetic  14.1 us (10%)
  local copies, waits for them, and re-layouts  11.3 us (8%)
  matrix products  11.1 us (8%)
  starting transfers between devices  3.54 us (2%)
    all_gather x1, blocking collectives, body(): lax.all_gather(factors, 'ctx', axis=0, tiled=True)  23.1 us
    all_gather x1, blocking collectives, body(): gathered_query = lax.all_gather(index_query, 'ctx', axis=0, tiled=True)  21.7 us
    all_gather x1, blocking collectives, body(): gathered_weight = lax.all_gather(index_weight, 'ctx', axis=0, tiled=True)  21.7 us
    all_gather x1, blocking collectives, body(): lax.all_gather(index_keys, 'ctx', axis=0, tiled=True)  20.3 us
    dot_general x4, matrix products, add_terms(): jnp.dot(grad_dots, key_rows, preferred_element_type=jnp.float32)  5.81 us
    reduce_sum x4, other arithmetic, add_terms(): target = jnp.sum(main_exp / main_total[:, :, None], axis=1) / head_count  4.73 us
    mul x1, local copies, waits for them, and re-layouts, dequantize(): scaled = scaled * factors.astype(jnp.float32)[:, :, None]  4.65 us
    dot_general x13, matrix products, dot_rows(): lax.dot_general(left, right, (((1,), (1,)), ((), ())), preferred_element_...  4.01 us
  transfers between devices with their start and end apart: 2, of which 0 were waited for; matrix products, arithmetic and copies ran while one was open for 2% of the time, Pallas kernels for 0%

commit v1 on v0

v1 whole, which is shorter than its diff:
```python
import jax
import jax.numpy as jnp
from jax import lax
from jax.sharding import PartitionSpec as P

ROPE = 64


main_scale = 192.0 ** (-0.5)


def dot_rows(left, right):
    return lax.dot_general(
        left, right, (((1,), (1,)), ((), ())), preferred_element_type=jnp.float32
    )


def dequantize(key_codes, key_scales):
    key_count = key_codes.shape[0]
    groups = key_scales.shape[1]
    group_width = (key_codes.shape[1] - ROPE) // groups
    factors = jnp.exp2(key_scales.astype(jnp.float32))
    scaled = key_codes[:, : groups * group_width].astype(jnp.float32)
    scaled = scaled.reshape(key_count, groups, group_width) * factors[:, :, None]
    rotary = key_codes[:, groups * group_width :].astype(jnp.float32)
    return jnp.concatenate([scaled.reshape(key_count, -1), rotary], axis=1).astype(jnp.bfloat16)


def swap(array, mask, count):
    return lax.ppermute(array, "ctx", [(i, i ^ mask) for i in range(count)])


def swap_gather(block, stride, parts, count):
    held = {0: block}
    bit = parts // 2
    while bit:
        held.update({k ^ bit: swap(own, stride * bit, count) for k, own in list(held.items())})
        bit //= 2
    return [held[k] for k in range(parts)]


def body(query_main, key_codes, key_scales, index_keys, index_query, index_weight, query_pos):
    own_rows, head_count, latent_width = query_main.shape
    index_heads, index_width = index_query.shape[1:]
    own_keys = key_codes.shape[0]
    count = lax.axis_size("ctx")
    row_parts = 4 if count % 4 == 0 else 1
    key_parts = count // row_parts
    me = lax.axis_index("ctx")
    key_total = own_keys * count
    index_scale = float(index_heads * index_width) ** (-0.5)
    rows = own_rows * row_parts
    keys = own_keys * key_parts

    latent = dequantize(key_codes, key_scales)
    key_pack = jnp.concatenate([latent, index_keys], axis=1)
    side = jnp.concatenate([index_weight, query_pos.astype(jnp.float32)[:, None]], axis=1)
    key_blocks = swap_gather(key_pack, row_parts, key_parts, count)
    query_blocks = swap_gather(query_main, 1, row_parts, count)
    iquery_blocks = swap_gather(index_query, 1, row_parts, count)
    side_blocks = swap_gather(side, 1, row_parts, count)

    key_all = jnp.concatenate(key_blocks, axis=0)
    latent_all = key_all[:, :latent_width]
    ikeys = key_all[:, latent_width:]
    main_flat = jnp.concatenate(query_blocks, axis=0).reshape(rows * head_count, latent_width)
    query_flat = jnp.concatenate(iquery_blocks, axis=0).reshape(rows * index_heads, index_width)
    side_all = jnp.concatenate(side_blocks, axis=0)
    weight = side_all[:, :index_heads]
    pos = side_all[:, index_heads].astype(jnp.int32)
    owners = jnp.stack([me ^ (row_parts * k) for k in range(key_parts)])
    key_pos = (owners[:, None] * own_keys + lax.iota(jnp.int32, own_keys)[None, :]).reshape(-1)
    visible = key_pos[None, :] <= pos[:, None]

    main_score = dot_rows(main_flat, latent_all).reshape(rows, head_count, keys) * main_scale
    main_exp = jnp.where(visible[:, None, :], jnp.exp(main_score), 0.0)
    head_dots = dot_rows(query_flat, ikeys).reshape(rows, index_heads, keys)
    positive = jnp.maximum(head_dots, 0.0)
    index_score = index_scale * jnp.sum(weight[:, :, None] * positive, axis=1)
    index_exp = jnp.where(visible, jnp.exp(index_score), 0.0)
    sums = jnp.concatenate(
        [jnp.sum(main_exp, axis=2), jnp.sum(index_exp, axis=1, keepdims=True)], axis=1
    )
    sums = sums.reshape(row_parts, own_rows, -1)
    bit = row_parts // 2
    while bit:
        got = swap(sums, bit, count)
        sums = sums + jnp.stack([got[r ^ bit] for r in range(row_parts)])
        bit //= 2
    sums = sums.reshape(rows, -1)
    main_total, index_total = sums[:, :head_count], sums[:, head_count:]

    target = jnp.sum(main_exp / main_total[:, :, None], axis=1) / head_count
    gradient = key_total * (index_exp / index_total - target)
    grad_weight = index_scale * jnp.sum(gradient[:, None, :] * positive, axis=2)
    grad_dots = jnp.where(
        head_dots > 0, index_scale * gradient[:, None, :] * weight[:, :, None], 0.0
    )
    grad_dots = grad_dots.astype(jnp.bfloat16).reshape(rows * index_heads, keys)
    key_part = lax.dot_general(
        grad_dots, query_flat, (((0,), (0,)), ((), ())), preferred_element_type=jnp.float32
    )
    key_part = key_part.reshape(key_parts, own_keys, index_width)
    got_keys = [
        swap(key_part[k].astype(jnp.bfloat16), row_parts * k, count) for k in range(1, key_parts)
    ]
    grad_query = jnp.dot(grad_dots, ikeys, preferred_element_type=jnp.float32)
    lines = own_rows * index_heads
    grad_rows = jnp.concatenate(
        [
            grad_query.reshape(row_parts, lines, index_width),
            grad_weight.reshape(row_parts, -1, index_width),
        ],
        axis=1,
    )
    bit = row_parts // 2
    while bit:
        grad_rows = grad_rows[:bit] + swap(grad_rows[bit:], bit, count)
        bit //= 2
    grad_rows = grad_rows[0]
    key_grad = key_part[0]
    for got in got_keys:
        key_grad = key_grad + got.astype(jnp.float32)
    return (
        grad_rows[:lines].reshape(own_rows, index_heads, index_width),
        grad_rows[lines:].reshape(own_rows, index_heads),
        key_grad,
    )


def solution(mesh):
    placed = (
        P(("grp", "ctx"), None, None),
        P(("grp", "ctx"), None),
        P(("grp", "ctx"), None),
        P(("grp", "ctx"), None),
        P(("grp", "ctx"), None, None),
        P(("grp", "ctx"), None),
        P(("grp", "ctx")),
    )
    return jax.shard_map(
        body,
        mesh=mesh,
        in_specs=placed,
        out_specs=(P(("grp", "ctx"), None, None), P(("grp", "ctx"), None), P(("grp", "ctx"), None)),
        check_vma=False,
    )
```

time: 142 us -> 52.1 us (0.37)
  blocking collectives: 86.8 us -> 0 us
  waiting for transfers between devices: 0.02 us -> 17.9 us
  starting transfers between devices: 3.54 us -> 19 us
  between operations: 14.2 us -> 0.98 us
  other arithmetic: 14.1 us -> 5 us
  matrix products: 11.1 us -> 3.66 us
  local copies, waits for them, and re-layouts: 11.3 us -> 5.29 us
    all_gather x4 -> x0, blocking collectives: 86.8 us -> none  [the longest x1 23.1 us: body(): lax.all_gather(factors, 'ctx', axis=0, tiled=True)]
    ppermute x0 -> x19, starting transfers between devices: none -> 19 us  [swap(): return lax.ppermute(array, 'ctx', [(i, i ^ mask) for i in range(count)])]
    ppermute x0 -> x19, waiting for transfers between devices: none -> 17.9 us  [swap(): return lax.ppermute(array, 'ctx', [(i, i ^ mask) for i in range(count)])]
    dot_general x5 -> x2, matrix products: 7.14 us -> 0.75 us  [the longest x1 0.46 us: body(): lax.dot_general(grad_dots, query_flat, (((0,), (0,)), ((), ())), preferre...]
    dynamic_update_slice x8 -> x0, other arithmetic: 6.26 us -> none  [the longest x4 3.55 us: add_norms(): lax.dynamic_update_slice_in_dim(main_store, main_exp, first_key, 2)]
    mul x6 -> x2, local copies, waits for them, and re-layouts: 5.75 us -> 0.27 us  [the longest x1 0.2 us: dequantize(): scaled.reshape(key_count, groups, group_width) * factors[:, :, None]]
    reduce_sum x8 -> x3, other arithmetic: 5.47 us -> 0.95 us  [the longest x1 0.59 us: body(): target = jnp.sum(main_exp / main_total[:, :, None], axis=1) / head_count]
    all_to_all x1 -> x0, starting transfers between devices: 3.5 us -> none  [body(): lax.all_to_all(buffer, 'ctx', split_axis=1, concat_axis=0, tiled=True)]
  transfers between devices with their start and end apart: 2 -> 19, of which waited for: 0 -> 7; matrix products, arithmetic and copies ran while one was open for 2% -> 10% of each run, Pallas kernels for 0% -> 0%
where the time goes in v1:
time: 52.1 us; the launch traced here: 51.8 us
  starting transfers between devices  19 us (36%)
  waiting for transfers between devices  17.9 us (34%)
  local copies, waits for them, and re-layouts  5.29 us (10%)
  other arithmetic  5 us (10%)
  matrix products  3.66 us (7%)
  between operations  0.98 us (2%)
    ppermute x19, starting transfers between devices, swap(): return lax.ppermute(array, 'ctx', [(i, i ^ mask) for i in range(count)])  19 us
    ppermute x19, waiting for transfers between devices, swap(): return lax.ppermute(array, 'ctx', [(i, i ^ mask) for i in range(count)])  17.9 us
    dot_general x2, matrix products, dot_rows(): lax.dot_general(left, right, (((1,), (1,)), ((), ())), preferred_element_...  2.9 us
    unnamed x27, local copies, waits for them, and re-layouts  1.55 us
  transfers between devices with their start and end apart: 19, of which 7 were waited for; matrix products, arithmetic and copies ran while one was open for 10% of the time, Pallas kernels for 0%

profile of v1, /device:TPU:0, one launch (start us, length us, event | category | flops | bytes accessed | tf_op | source)
XLA Modules:
  0.0 51.8 jit_solution(10725928785288808596)
XLA Ops:
  0.7 0.7 %convert_bitcast_fusion = f32[2,1]{0,1:T(1,128)S(1)} fusion(s32[2]{0:T(128)} %param.13), kind=kLoop, calls=%fused_computation.62 | loop fusion | flops 2 | bytes 16 | tf_op jit(solution)/shard_map/broadcast_in_dim | solution.py:57
  1.4 0.1 copy.26
  1.5 0.8 %pad_maximum_fusion.15 = f32[2,65]{1,0:T(2,128)S(1)} fusion(f32[2,1]{1,0:T(2,128)S(1)} %copy.26, f32[2,64]{1,0:T(2,128)} %param.12), kind=kLoop, calls=%fused_computation.59 | loop fusion | flops 130 | bytes 1040 | tf_op jit(solution)/shard_map/concatenate | solution.py:57
  2.2 3.0 %collective-permute-start.7 = (f32[2,65]{1,0:T(2,128)S(1)}, f32[2,65]{1,0:T(2,128)S(1)}, u32[]{:S(2)}, u32[]{:S(2)}) collective-permute-start(f32[2,65]{1,0:T(2,128)S(1)} %pad_maximum_fusion.15), channel_id=1, source_target_pairs={{0,2},{1,3},{2,0},{3,1},{4,6},{5,7},{6,4},{7,5},{8,10},{9,11},{10,... | collective-permute-start | bytes 1568 | tf_op jit(solution)/shard_map/ppermute | solution.py:30
  5.2 0.5 collective-permute-start
  5.7 0.7 %slice.86 = bf16[128,64]{0,1:T(8,128)(2,1)S(1)} slice(bf16[128,576]{0,1:T(8,128)(2,1)} %param.8), slice={[0:128], [512:576]} | slice | bytes 32768 | tf_op jit(solution)/shard_map/slice | solution.py:25
  6.4 0.9 %slice.85 = bf16[128,512]{0,1:T(8,128)(2,1)S(1)} slice(bf16[128,576]{0,1:T(8,128)(2,1)} %param.8), slice={[0:128], [0:512]} | slice | bytes 262144 | tf_op jit(solution)/shard_map/slice | solution.py:23
  7.3 0.7 %multiply_exponential_fusion = f32[128,4]{0,1:T(4,128)S(1)} fusion(s32[128,4]{0,1:T(4,128)} %param.9), kind=kLoop, calls=%fused_computation.58 | loop fusion | flops 1024 | bytes 4096 | tf_op jit(solution)/shard_map/exp2 | solution.py:22
  8.0 0.1 copy.33
  8.2 0.1 copy.24
  8.3 0.1 copy.32
  8.4 0.2 mul.103
  8.6 0.1 pad_maximum_fusion.9
  8.7 3.2 %collective-permute-start.4 = (bf16[128,704]{1,0:T(8,128)(2,1)S(1)}, bf16[128,704]{1,0:T(8,128)(2,1)S(1)}, u32[]{:S(2)}, u32[]{:S(2)}) collective-permute-start(bf16[128,704]{1,0:T(8,128)(2,1)S(1)} %pad_maximum_fusion.9), channel_id=1, source_target_pairs={{0,8},{1,9},{2,10},{3,11},{4,12},{5,13},{6,14},{7,15},{8,0},{9,1},... | collective-permute-start | bytes 540680 | tf_op jit(solution)/shard_map/ppermute | solution.py:30
  12.1 1.6 %collective-permute-start.3 = (bf16[128,704]{1,0:T(8,128)(2,1)S(1)}, bf16[128,704]{1,0:T(8,128)(2,1)S(1)}, u32[]{:S(2)}, u32[]{:S(2)}) collective-permute-start(bf16[128,704]{1,0:T(8,128)(2,1)S(1)} %pad_maximum_fusion.9), channel_id=1, source_target_pairs={{0,4},{1,5},{2,6},{3,7},{4,0},{5,1},{6,2},{7,3},{8,12},{9,13},{10,... | collective-permute-start | bytes 540680 | tf_op jit(solution)/shard_map/ppermute | solution.py:30
  13.8 0.2 collective-permute-start.9
  14.1 0.2 convert_reduce_fusion
  14.3 1.5 %collective-permute-start.10 = (bf16[2,128,576]{1,2,0:T(8,128)(2,1)S(1)}, bf16[2,128,576]{1,2,0:T(8,128)(2,1)S(1)}, u32[]{:S(2)}, u32[]{:S(2)}) collective-permute-start(bf16[2,128,576]{1,2,0:T(8,128)(2,1)S(1)} %copy-done.8), channel_id=1, source_target_pairs={{0,2},{1,3},{2,0},{3,1},{4,6},{5,7},{6,4},{7,5},{8,10},{9,11},{10,... | collective-permute-start | bytes 884744 | tf_op jit(solution)/shard_map/ppermute | solution.py:30
  15.9 5.2 %collective-permute-done.4 = bf16[128,704]{1,0:T(8,128)(2,1)S(1)} collective-permute-done((bf16[128,704]{1,0:T(8,128)(2,1)S(1)}, bf16[128,704]{1,0:T(8,128)(2,1)S(1)}, u32[]{:S(2)}, u32[]{:S(2)}) %collective-permute-start.4) | collective-permute-done | bytes 180256 | tf_op jit(solution)/shard_map/ppermute | solution.py:30
  21.0 0.7 %collective-permute-start.5 = (bf16[128,704]{1,0:T(8,128)(2,1)S(1)}, bf16[128,704]{1,0:T(8,128)(2,1)S(1)}, u32[]{:S(2)}, u32[]{:S(2)}) collective-permute-start(bf16[128,704]{1,0:T(8,128)(2,1)S(1)} %collective-permute-done.4), channel_id=1, source_target_pairs={{0,4},{1,5},{2,6},{3,7},{4,0},{5,1},{6,2},{7,3},{8,12},{9,13},{10,... | collective-permute-start | bytes 540680 | tf_op jit(solution)/shard_map/ppermute | solution.py:30
  21.7 1.8 %collective-permute-done.10 = bf16[2,128,576]{1,2,0:T(8,128)(2,1)S(1)} collective-permute-done((bf16[2,128,576]{1,2,0:T(8,128)(2,1)S(1)}, bf16[2,128,576]{1,2,0:T(8,128)(2,1)S(1)}, u32[]{:S(2)}, u32[]{:S(2)}) %collective-permute-start.10) | collective-permute-done | bytes 294944 | tf_op jit(solution)/shard_map/ppermute | solution.py:30
  23.6 3.3 %collective-permute-done.5 = bf16[128,704]{1,0:T(8,128)(2,1)S(1)} collective-permute-done((bf16[128,704]{1,0:T(8,128)(2,1)S(1)}, bf16[128,704]{1,0:T(8,128)(2,1)S(1)}, u32[]{:S(2)}, u32[]{:S(2)}) %collective-permute-start.5) | collective-permute-done | bytes 180256 | tf_op jit(solution)/shard_map/ppermute | solution.py:30
  26.9 0.1 maximum_bitcast_fusion
  27.0 0.5 %copy-done.4 = bf16[128,704]{1,0:T(8,128)(2,1)} copy-done((bf16[128,704]{1,0:T(8,128)(2,1)}, bf16[128,704]{1,0:T(8,128)(2,1)S(1)}, u32[]{:S(2)}) %copy-start.4) | copy-done | bytes 180248
  27.6 0.3 multiply_reduce_fusion.1
  27.9 0.2 fusion.18
  28.1 0.1 concatenate.53
  28.2 0.7 %copy-done.9 = bf16[2,128,576]{1,2,0:T(8,128)(2,1)} copy-done((bf16[2,128,576]{1,2,0:T(8,128)(2,1)}, bf16[2,128,576]{1,2,0:T(8,128)(2,1)S(1)}, u32[]{:S(2)}) %copy-start.9) | copy-done | bytes 294936
  28.9 2.6 %fusion = (f32[8,128]{1,0:T(8,128)S(1)}, f32[8,128,512]{2,1,0:T(8,128)S(1)}) fusion(pred[8,512]{1,0:T(8,128)(4,1)S(1)} %broadcast_compare_fusion, bf16[128,704]{1,0:T(8,128)(2,1)} %copy-done.4, bf16[128,704]{1,0:T(8,128)(2,1)} %copy-done.2, bf16[128,704]{1,0:T(8,128)(2,1)} %copy-done.3, bf16[128,128]{1,0:T(8,128)(2,1)S(1)} %copy-done.5, ...), kind=kOutput, calls=%fused_computation.2 | convolution fusion | flops 610860032 | bytes 4005888 | tf_op jit(solution)/shard_map/dot_general | solution.py:13
  31.5 1.5 %collective-permute-start.12 = (f32[4,2,129]{2,1,0:T(2,128)S(1)}, f32[4,2,129]{2,1,0:T(2,128)S(1)}, u32[]{:S(2)}, u32[]{:S(2)}) collective-permute-start(f32[4,2,129]{2,1,0:T(2,128)S(1)} %pad_maximum_fusion.11), channel_id=1, source_target_pairs={{0,2},{1,3},{2,0},{3,1},{4,6},{5,7},{6,4},{7,5},{8,10},{9,11},{10,... | collective-permute-start | bytes 12392 | tf_op jit(solution)/shard_map/ppermute | solution.py:30
  33.0 2.2 %collective-permute-done.12 = f32[4,2,129]{2,1,0:T(2,128)S(1)} collective-permute-done((f32[4,2,129]{2,1,0:T(2,128)S(1)}, f32[4,2,129]{2,1,0:T(2,128)S(1)}, u32[]{:S(2)}, u32[]{:S(2)}) %collective-permute-start.12) | collective-permute-done | bytes 4160 | tf_op jit(solution)/shard_map/ppermute | solution.py:30
  35.3 0.1 fusion.12
  35.6 0.9 %collective-permute-done.13 = f32[4,2,129]{2,1,0:T(2,128)S(1)} collective-permute-done((f32[4,2,129]{2,1,0:T(2,128)S(1)}, f32[4,2,129]{2,1,0:T(2,128)S(1)}, u32[]{:S(2)}, u32[]{:S(2)}) %collective-permute-start.13) | collective-permute-done | bytes 4160 | tf_op jit(solution)/shard_map/ppermute | solution.py:30
  36.5 0.1 slice_reduce_fusion
  36.6 0.6 %divide_reduce_fusion = f32[8,512]{1,0:T(8,128)S(1)} fusion(f32[8,128,512]{2,1,0:T(8,128)S(1)} %get-tuple-element.19, f32[8,128]{1,0:T(8,128)S(1)} %slice.116, pred[8,512]{1,0:T(8,128)(4,1)S(1)} %broadcast_compare_fusion), kind=kLoop, calls=%fused_computation.1 | loop fusion | flops 2093056 | bytes 2121728 | tf_op jit(solution)/shard_map/reduce_sum | solution.py:93
  37.3 0.5 fusion.25
  37.8 0.2 select_convert_fusion
  38.0 0.2 multiply_reduce_fusion
  38.3 0.3 fusion.26
  38.6 1.5 %collective-permute-start.14 = (f32[2,129,128]{2,1,0:T(8,128)S(1)}, f32[2,129,128]{2,1,0:T(8,128)S(1)}, u32[]{:S(2)}, u32[]{:S(2)}) collective-permute-start(f32[2,129,128]{2,1,0:T(8,128)S(1)} %pad_maximum_fusion.10), channel_id=1, source_target_pairs={{0,2},{1,3},{2,0},{3,1},{4,6},{5,7},{6,4},{7,5},{8,10},{9,11},{10,... | collective-permute-start | bytes 396296 | tf_op jit(solution)/shard_map/ppermute | solution.py:30
  40.1 1.8 %collective-permute-start.16 = (bf16[128,128]{1,0:T(8,128)(2,1)S(1)}, bf16[128,128]{1,0:T(8,128)(2,1)S(1)}, u32[]{:S(2)}, u32[]{:S(2)}) collective-permute-start(bf16[128,128]{1,0:T(8,128)(2,1)S(1)} %get-tuple-element.5), channel_id=1, source_target_pairs={{0,4},{1,5},{2,6},{3,7},{4,0},{5,1},{6,2},{7,3},{8,12},{9,13},{10,... | collective-permute-start | bytes 98312 | tf_op jit(solution)/shard_map/ppermute | solution.py:30
  41.9 3.1 %collective-permute-start.18 = (bf16[128,128]{1,0:T(8,128)(2,1)S(1)}, bf16[128,128]{1,0:T(8,128)(2,1)S(1)}, u32[]{:S(2)}, u32[]{:S(2)}) collective-permute-start(bf16[128,128]{1,0:T(8,128)(2,1)S(1)} %get-tuple-element.6), channel_id=1, source_target_pairs={{0,12},{1,13},{2,14},{3,15},{4,8},{5,9},{6,10},{7,11},{8,4},{9,5},... | collective-permute-start | bytes 98312 | tf_op jit(solution)/shard_map/ppermute | solution.py:30
  45.0 0.3 collective-permute-start.17
  45.4 2.2 %collective-permute-done.18 = bf16[128,128]{1,0:T(8,128)(2,1)S(1)} collective-permute-done((bf16[128,128]{1,0:T(8,128)(2,1)S(1)}, bf16[128,128]{1,0:T(8,128)(2,1)S(1)}, u32[]{:S(2)}, u32[]{:S(2)}) %collective-permute-start.18) | collective-permute-done | bytes 32800 | tf_op jit(solution)/shard_map/ppermute | solution.py:30
  47.6 2.2 %collective-permute-done.17 = bf16[128,128]{1,0:T(8,128)(2,1)S(1)} collective-permute-done((bf16[128,128]{1,0:T(8,128)(2,1)S(1)}, bf16[128,128]{1,0:T(8,128)(2,1)S(1)}, u32[]{:S(2)}, u32[]{:S(2)}) %collective-permute-start.17) | collective-permute-done | bytes 32800 | tf_op jit(solution)/shard_map/ppermute | solution.py:30
  49.8 0.6 %fusion.17 = f32[128,128]{1,0:T(8,128)} fusion(f32[512,128]{1,0:T(8,128)S(1)} %get-tuple-element.21, bf16[128,128]{1,0:T(8,128)(2,1)S(1)} %collective-permute-done.18, bf16[128,128]{1,0:T(8,128)(2,1)S(1)} %collective-permute-done.17, bf16[128,128]{1,0:T(8,128)(2,1)S(1)} %collective-permute-done.16), kind=kLoop, calls=%fused_computation.37 | loop fusion | flops 98304 | bytes 229376 | tf_op jit(solution)/shard_map/add | solution.py:123
  50.5 0.6 %slice.121 = f32[1,128,128]{2,1,0:T(8,128)} slice(f32[1,129,128]{2,1,0:T(8,128)S(1)} %slice_add_fusion), slice={[0:1], [0:128], [0:128]} | slice | bytes 131072 | tf_op jit(solution)/shard_map/slice | solution.py:125
  51.1 0.6 %reshape.227 = f32[2,64]{1,0:T(2,128)} reshape(f32[128]{0:T(128)S(1)} %slice_reduce_fusion.1) | data formatting | bytes 1024 | tf_op jit(solution)/shard_map/reshape | solution.py:126
  (68 shorter events, 1.0 us)
Async XLA Ops:
  0.6 13.3 %copy-start.7 = (f32[2,64]{1,0:T(2,128)S(1)}, f32[2,64]{1,0:T(2,128)}, u32[]{:S(2)}) copy-start(f32[2,64]{1,0:T(2,128)} %param.12) | copy-start | bytes 1540
  0.6 11.5 %copy-start.6 = (bf16[2,64,128]{2,1,0:T(8,128)(2,1)S(1)}, bf16[2,64,128]{2,1,0:T(8,128)(2,1)}, u32[]{:S(2)}) copy-start(bf16[2,64,128]{2,1,0:T(8,128)(2,1)} %param.11) | copy-start | bytes 98308
  0.7 8.0 %copy-start.5 = (bf16[128,128]{1,0:T(8,128)(2,1)S(1)}, bf16[128,128]{1,0:T(8,128)(2,1)}, u32[]{:S(2)}) copy-start(bf16[128,128]{1,0:T(8,128)(2,1)} %param.10) | copy-start | bytes 98308
  0.7 13.1 %copy-start.8 = (bf16[2,128,576]{1,2,0:T(8,128)(2,1)S(1)}, bf16[2,128,576]{1,2,0:T(8,128)(2,1)}, u32[]{:S(2)}) copy-start(bf16[2,128,576]{1,2,0:T(8,128)(2,1)} %param.7) | copy-start | bytes 884740
  2.2 9.8 %collective-permute-start.7 = (f32[2,65]{1,0:T(2,128)S(1)}, f32[2,65]{1,0:T(2,128)S(1)}, u32[]{:S(2)}, u32[]{:S(2)}) collective-permute-start(f32[2,65]{1,0:T(2,128)S(1)} %pad_maximum_fusion.15), channel_id=1, source_target_pairs={{0,2},{1,3},{2,0},{3,1},{4,6},{5,7},{6,4},{7,5},{8,10},{9,11},{10,... | collective-permute-start | bytes 1568 | tf_op jit(solution)/shard_map/ppermute | solution.py:30
  5.2 6.9 %collective-permute-start.6 = (f32[2,65]{1,0:T(2,128)S(1)}, f32[2,65]{1,0:T(2,128)S(1)}, u32[]{:S(2)}, u32[]{:S(2)}) collective-permute-start(f32[2,65]{1,0:T(2,128)S(1)} %pad_maximum_fusion.15), channel_id=1, source_target_pairs={{0,1},{1,0},{2,3},{3,2},{4,5},{5,4},{6,7},{7,6},{8,9},{9,8},{10,11... | collective-permute-start | bytes 1568 | tf_op jit(solution)/shard_map/ppermute | solution.py:30
  5.2 9.1 %collective-permute-start = (bf16[2,64,128]{2,1,0:T(8,128)(2,1)}, bf16[2,64,128]{2,1,0:T(8,128)(2,1)S(1)}, u32[]{:S(2)}, u32[]{:S(2)}) collective-permute-start(bf16[2,64,128]{2,1,0:T(8,128)(2,1)} %param.11), channel_id=1, source_target_pairs={{0,1},{1,0},{2,3},{3,2},{4,5},{5,4},{6,7},{7,6},{8,9},{9,8},{10,11... | collective-permute-start | bytes 98312 | tf_op jit(solution)/shard_map/ppermute | solution.py:30
  5.7 10.1 %collective-permute-start.1 = (bf16[2,64,128]{2,1,0:T(8,128)(2,1)}, bf16[2,64,128]{2,1,0:T(8,128)(2,1)S(1)}, u32[]{:S(2)}, u32[]{:S(2)}) collective-permute-start(bf16[2,64,128]{2,1,0:T(8,128)(2,1)} %param.11), channel_id=1, source_target_pairs={{0,2},{1,3},{2,0},{3,1},{4,6},{5,7},{6,4},{7,5},{8,10},{9,11},{10,... | collective-permute-start | bytes 98312 | tf_op jit(solution)/shard_map/ppermute | solution.py:30
  8.7 12.3 %collective-permute-start.4 = (bf16[128,704]{1,0:T(8,128)(2,1)S(1)}, bf16[128,704]{1,0:T(8,128)(2,1)S(1)}, u32[]{:S(2)}, u32[]{:S(2)}) collective-permute-start(bf16[128,704]{1,0:T(8,128)(2,1)S(1)} %pad_maximum_fusion.9), channel_id=1, source_target_pairs={{0,8},{1,9},{2,10},{3,11},{4,12},{5,13},{6,14},{7,15},{8,0},{9,1},... | collective-permute-start | bytes 540680 | tf_op jit(solution)/shard_map/ppermute | solution.py:30
  12.1 1.7 %collective-permute-start.8 = (f32[2,65]{1,0:T(2,128)S(1)}, f32[2,65]{1,0:T(2,128)S(1)}, u32[]{:S(2)}, u32[]{:S(2)}) collective-permute-start(f32[2,65]{1,0:T(2,128)S(1)} %collective-permute-done.7), channel_id=1, source_target_pairs={{0,1},{1,0},{2,3},{3,2},{4,5},{5,4},{6,7},{7,6},{8,9},{9,8},{10,11... | collective-permute-start | bytes 1568 | tf_op jit(solution)/shard_map/ppermute | solution.py:30
  12.1 11.4 %collective-permute-start.3 = (bf16[128,704]{1,0:T(8,128)(2,1)S(1)}, bf16[128,704]{1,0:T(8,128)(2,1)S(1)}, u32[]{:S(2)}, u32[]{:S(2)}) collective-permute-start(bf16[128,704]{1,0:T(8,128)(2,1)S(1)} %pad_maximum_fusion.9), channel_id=1, source_target_pairs={{0,4},{1,5},{2,6},{3,7},{4,0},{5,1},{6,2},{7,3},{8,12},{9,13},{10,... | collective-permute-start | bytes 540680 | tf_op jit(solution)/shard_map/ppermute | solution.py:30
  13.8 14.4 %collective-permute-start.9 = (bf16[2,128,576]{1,2,0:T(8,128)(2,1)S(1)}, bf16[2,128,576]{1,2,0:T(8,128)(2,1)S(1)}, u32[]{:S(2)}, u32[]{:S(2)}) collective-permute-start(bf16[2,128,576]{1,2,0:T(8,128)(2,1)S(1)} %copy-done.8), channel_id=1, source_target_pairs={{0,1},{1,0},{2,3},{3,2},{4,5},{5,4},{6,7},{7,6},{8,9},{9,8},{10,11... | collective-permute-start | bytes 884744 | tf_op jit(solution)/shard_map/ppermute | solution.py:30
  14.3 9.2 %collective-permute-start.10 = (bf16[2,128,576]{1,2,0:T(8,128)(2,1)S(1)}, bf16[2,128,576]{1,2,0:T(8,128)(2,1)S(1)}, u32[]{:S(2)}, u32[]{:S(2)}) collective-permute-start(bf16[2,128,576]{1,2,0:T(8,128)(2,1)S(1)} %copy-done.8), channel_id=1, source_target_pairs={{0,2},{1,3},{2,0},{3,1},{4,6},{5,7},{6,4},{7,5},{8,10},{9,11},{10,... | collective-permute-start | bytes 884744 | tf_op jit(solution)/shard_map/ppermute | solution.py:30
  15.8 5.9 %collective-permute-start.2 = (bf16[2,64,128]{2,1,0:T(8,128)(2,1)S(1)}, bf16[2,64,128]{2,1,0:T(8,128)(2,1)S(1)}, u32[]{:S(2)}, u32[]{:S(2)}) collective-permute-start(bf16[2,64,128]{2,1,0:T(8,128)(2,1)S(1)} %collective-permute-done.1), channel_id=1, source_target_pairs={{0,1},{1,0},{2,3},{3,2},{4,5},{5,4},{6,7},{7,6},{8,9},{9,8},{10,11... | collective-permute-start | bytes 98312 | tf_op jit(solution)/shard_map/ppermute | solution.py:30
  21.0 6.0 %copy-start.2 = (bf16[128,704]{1,0:T(8,128)(2,1)}, bf16[128,704]{1,0:T(8,128)(2,1)S(1)}, u32[]{:S(2)}) copy-start(bf16[128,704]{1,0:T(8,128)(2,1)S(1)} %collective-permute-done.4) | copy-start | bytes 540676
  21.0 5.8 %collective-permute-start.5 = (bf16[128,704]{1,0:T(8,128)(2,1)S(1)}, bf16[128,704]{1,0:T(8,128)(2,1)S(1)}, u32[]{:S(2)}, u32[]{:S(2)}) collective-permute-start(bf16[128,704]{1,0:T(8,128)(2,1)S(1)} %collective-permute-done.4), channel_id=1, source_target_pairs={{0,4},{1,5},{2,6},{3,7},{4,0},{5,1},{6,2},{7,3},{8,12},{9,13},{10,... | collective-permute-start | bytes 540680 | tf_op jit(solution)/shard_map/ppermute | solution.py:30
  21.7 6.4 %copy-start = (bf16[8,64,128]{2,1,0:T(8,128)(2,1)}, bf16[8,64,128]{2,1,0:T(8,128)(2,1)S(1)}, u32[]{:S(2)}) copy-start(bf16[8,64,128]{2,1,0:T(8,128)(2,1)S(1)} %constant_dynamic-update-slice_fusion) | copy-start | bytes 393220
  23.5 4.6 %copy-start.10 = (bf16[2,128,576]{1,2,0:T(8,128)(2,1)}, bf16[2,128,576]{1,2,0:T(8,128)(2,1)S(1)}, u32[]{:S(2)}) copy-start(bf16[2,128,576]{1,2,0:T(8,128)(2,1)S(1)} %collective-permute-done.10) | copy-start | bytes 884740
  23.6 5.3 %collective-permute-start.11 = (bf16[2,128,576]{1,2,0:T(8,128)(2,1)S(1)}, bf16[2,128,576]{1,2,0:T(8,128)(2,1)}, u32[]{:S(2)}, u32[]{:S(2)}) collective-permute-start(bf16[2,128,576]{1,2,0:T(8,128)(2,1)S(1)} %collective-permute-done.10), channel_id=1, source_target_pairs={{0,1},{1,0},{2,3},{3,2},{4,5},{5,4},{6,7},{7,6},{8,9},{9,8},{10,11... | collective-permute-start | bytes 884744 | tf_op jit(solution)/shard_map/ppermute | solution.py:30
  23.6 3.4 %copy-start.3 = (bf16[128,704]{1,0:T(8,128)(2,1)}, bf16[128,704]{1,0:T(8,128)(2,1)S(1)}, u32[]{:S(2)}) copy-start(bf16[128,704]{1,0:T(8,128)(2,1)S(1)} %collective-permute-done.3) | copy-start | bytes 540676
  26.9 0.7 %copy-start.4 = (bf16[128,704]{1,0:T(8,128)(2,1)}, bf16[128,704]{1,0:T(8,128)(2,1)S(1)}, u32[]{:S(2)}) copy-start(bf16[128,704]{1,0:T(8,128)(2,1)S(1)} %collective-permute-done.5) | copy-start | bytes 540676
  28.2 0.7 %copy-start.9 = (bf16[2,128,576]{1,2,0:T(8,128)(2,1)}, bf16[2,128,576]{1,2,0:T(8,128)(2,1)S(1)}, u32[]{:S(2)}) copy-start(bf16[2,128,576]{1,2,0:T(8,128)(2,1)S(1)} %collective-permute-done.9) | copy-start | bytes 884740
  31.5 3.7 %collective-permute-start.12 = (f32[4,2,129]{2,1,0:T(2,128)S(1)}, f32[4,2,129]{2,1,0:T(2,128)S(1)}, u32[]{:S(2)}, u32[]{:S(2)}) collective-permute-start(f32[4,2,129]{2,1,0:T(2,128)S(1)} %pad_maximum_fusion.11), channel_id=1, source_target_pairs={{0,2},{1,3},{2,0},{3,1},{4,6},{5,7},{6,4},{7,5},{8,10},{9,11},{10,... | collective-permute-start | bytes 12392 | tf_op jit(solution)/shard_map/ppermute | solution.py:30
  35.2 1.2 %collective-permute-start.13 = (f32[4,2,129]{2,1,0:T(2,128)S(1)}, f32[4,2,129]{2,1,0:T(2,128)S(1)}, u32[]{:S(2)}, u32[]{:S(2)}) collective-permute-start(f32[4,2,129]{2,1,0:T(2,128)S(1)} %get-tuple-element.9), channel_id=1, source_target_pairs={{0,1},{1,0},{2,3},{3,2},{4,5},{5,4},{6,7},{7,6},{8,9},{9,8},{10,11... | collective-permute-start | bytes 12392 | tf_op jit(solution)/shard_map/ppermute | solution.py:30
  35.5 1.8 %copy-start.1 = (bf16[8,64,128]{2,1,0:T(8,128)(2,1)S(1)}, bf16[8,64,128]{2,1,0:T(8,128)(2,1)}, u32[]{:S(2)}) copy-start(bf16[8,64,128]{2,1,0:T(8,128)(2,1)} %copy-done) | copy-start | bytes 393220
  38.6 6.6 %collective-permute-start.14 = (f32[2,129,128]{2,1,0:T(8,128)S(1)}, f32[2,129,128]{2,1,0:T(8,128)S(1)}, u32[]{:S(2)}, u32[]{:S(2)}) collective-permute-start(f32[2,129,128]{2,1,0:T(8,128)S(1)} %pad_maximum_fusion.10), channel_id=1, source_target_pairs={{0,2},{1,3},{2,0},{3,1},{4,6},{5,7},{6,4},{7,5},{8,10},{9,11},{10,... | collective-permute-start | bytes 396296 | tf_op jit(solution)/shard_map/ppermute | solution.py:30
  40.1 5.3 %collective-permute-start.16 = (bf16[128,128]{1,0:T(8,128)(2,1)S(1)}, bf16[128,128]{1,0:T(8,128)(2,1)S(1)}, u32[]{:S(2)}, u32[]{:S(2)}) collective-permute-start(bf16[128,128]{1,0:T(8,128)(2,1)S(1)} %get-tuple-element.5), channel_id=1, source_target_pairs={{0,4},{1,5},{2,6},{3,7},{4,0},{5,1},{6,2},{7,3},{8,12},{9,13},{10,... | collective-permute-start | bytes 98312 | tf_op jit(solution)/shard_map/ppermute | solution.py:30
  41.9 5.7 %collective-permute-start.18 = (bf16[128,128]{1,0:T(8,128)(2,1)S(1)}, bf16[128,128]{1,0:T(8,128)(2,1)S(1)}, u32[]{:S(2)}, u32[]{:S(2)}) collective-permute-start(bf16[128,128]{1,0:T(8,128)(2,1)S(1)} %get-tuple-element.6), channel_id=1, source_target_pairs={{0,12},{1,13},{2,14},{3,15},{4,8},{5,9},{6,10},{7,11},{8,4},{9,5},... | collective-permute-start | bytes 98312 | tf_op jit(solution)/shard_map/ppermute | solution.py:30
  45.0 4.8 %collective-permute-start.17 = (bf16[128,128]{1,0:T(8,128)(2,1)S(1)}, bf16[128,128]{1,0:T(8,128)(2,1)S(1)}, u32[]{:S(2)}, u32[]{:S(2)}) collective-permute-start(bf16[128,128]{1,0:T(8,128)(2,1)S(1)} %get-tuple-element.7), channel_id=1, source_target_pairs={{0,8},{1,9},{2,10},{3,11},{4,12},{5,13},{6,14},{7,15},{8,0},{9,1},... | collective-permute-start | bytes 98312 | tf_op jit(solution)/shard_map/ppermute | solution.py:30
  45.3 5.2 %collective-permute-start.15 = (f32[1,129,128]{2,1,0:T(8,128)S(1)}, f32[1,129,128]{2,1,0:T(8,128)S(1)}, u32[]{:S(2)}, u32[]{:S(2)}) collective-permute-start(f32[1,129,128]{2,1,0:T(8,128)S(1)} %slice.120), channel_id=1, source_target_pairs={{0,1},{1,0},{2,3},{3,2},{4,5},{5,4},{6,7},{7,6},{8,9},{9,8},{10,11... | collective-permute-start | bytes 198152 | tf_op jit(solution)/shard_map/ppermute | solution.py:30

commit v2 on v1

--- a/solution.py
+++ b/solution.py
@@ -1,6 +1,8 @@
 import jax
 import jax.numpy as jnp
 from jax import lax
+from jax.experimental import pallas as pl
+from jax.experimental.pallas import tpu as pltpu
 from jax.sharding import PartitionSpec as P
 
 ROPE = 64
@@ -15,15 +17,26 @@
     )
 
 
-def dequantize(key_codes, key_scales):
-    key_count = key_codes.shape[0]
-    groups = key_scales.shape[1]
-    group_width = (key_codes.shape[1] - ROPE) // groups
-    factors = jnp.exp2(key_scales.astype(jnp.float32))
-    scaled = key_codes[:, : groups * group_width].astype(jnp.float32)
-    scaled = scaled.reshape(key_count, groups, group_width) * factors[:, :, None]
-    rotary = key_codes[:, groups * group_width :].astype(jnp.float32)
-    return jnp.concatenate([scaled.reshape(key_count, -1), rotary], axis=1).astype(jnp.bfloat16)
+def pack_kernel(codes_ref, scales_ref, keys_ref, out_ref):
+    groups = scales_ref.shape[0]
+    latent_width = codes_ref.shape[0]
+    group_width = (latent_width - ROPE) // groups
+    factors = jnp.exp2(scales_ref[...].astype(jnp.float32))
+    for g in range(groups):
+        lines = slice(g * group_width, (g + 1) * group_width)
+        scaled = codes_ref[lines, :].astype(jnp.float32) * factors[g : g + 1, :]
+        out_ref[lines, :] = scaled.astype(jnp.bfloat16)
+    out_ref[groups * group_width : latent_width, :] = codes_ref[groups * group_width :, :]
+    out_ref[latent_width:, :] = keys_ref[...]
+
+
+def pack_keys(codes, scales, index_keys):
+    lines = codes.shape[0] + index_keys.shape[0]
+    return pl.pallas_call(
+        pack_kernel,
+        out_shape=jax.ShapeDtypeStruct((lines, codes.shape[1]), jnp.bfloat16),
+        name="pack_keys",
+    )(codes, scales, index_keys)
 
 
 def swap(array, mask, count):
@@ -52,17 +65,18 @@
     rows = own_rows * row_parts
     keys = own_keys * key_parts
 
-    latent = dequantize(key_codes, key_scales)
-    key_pack = jnp.concatenate([latent, index_keys], axis=1)
+    key_pack = pack_keys(key_codes.T, key_scales.T, index_keys)
+    key_pack, query_main, index_query, index_weight, query_pos = lax.optimization_barrier(
+        (key_pack, query_main, index_query, index_weight, query_pos)
+    )
+    key_blocks = swap_gather(key_pack, row_parts, key_parts, count)
     side = jnp.concatenate([index_weight, query_pos.astype(jnp.float32)[:, None]], axis=1)
-    key_blocks = swap_gather(key_pack, row_parts, key_parts, count)
     query_blocks = swap_gather(query_main, 1, row_parts, count)
     iquery_blocks = swap_gather(index_query, 1, row_parts, count)
     side_blocks = swap_gather(side, 1, row_parts, count)
 
-    key_all = jnp.concatenate(key_blocks, axis=0)
-    latent_all = key_all[:, :latent_width]
-    ikeys = key_all[:, latent_width:]
+    latent_all = jnp.concatenate([b[:latent_width] for b in key_blocks], axis=1)
+    ikeys = jnp.concatenate([b[latent_width:] for b in key_blocks], axis=0)
     main_flat = jnp.concatenate(query_blocks, axis=0).reshape(rows * head_count, latent_width)
     query_flat = jnp.concatenate(iquery_blocks, axis=0).reshape(rows * index_heads, index_width)
     side_all = jnp.concatenate(side_blocks, axis=0)
@@ -72,7 +86,7 @@
     key_pos = (owners[:, None] * own_keys + lax.iota(jnp.int32, own_keys)[None, :]).reshape(-1)
     visible = key_pos[None, :] <= pos[:, None]
 
-    main_score = dot_rows(main_flat, latent_all).reshape(rows, head_count, keys) * main_scale
+    main_score = jnp.dot(main_flat, latent_all, preferred_element_type=jnp.float32).reshape(rows, head_count, keys) * main_scale
     main_exp = jnp.where(visible[:, None, :], jnp.exp(main_score), 0.0)
     head_dots = dot_rows(query_flat, ikeys).reshape(rows, index_heads, keys)
     positive = jnp.maximum(head_dots, 0.0)
@@ -101,9 +115,16 @@
         grad_dots, query_flat, (((0,), (0,)), ((), ())), preferred_element_type=jnp.float32
     )
     key_part = key_part.reshape(key_parts, own_keys, index_width)
-    got_keys = [
-        swap(key_part[k].astype(jnp.bfloat16), row_parts * k, count) for k in range(1, key_parts)
-    ]
+    halves = key_part[key_parts // 2 :].astype(jnp.bfloat16)
+    key_sum = key_part[: key_parts // 2]
+    bit = key_parts // 2
+    while bit:
+        key_sum = key_sum + swap(halves, row_parts * bit, count).astype(jnp.float32)
+        bit //= 2
+        if bit:
+            halves = key_sum[bit:].astype(jnp.bfloat16)
+            key_sum = key_sum[:bit]
+    key_grad = key_sum[0]
     grad_query = jnp.dot(grad_dots, ikeys, preferred_element_type=jnp.float32)
     lines = own_rows * index_heads
     grad_rows = jnp.concatenate(
@@ -118,9 +139,6 @@
         grad_rows = grad_rows[:bit] + swap(grad_rows[bit:], bit, count)
         bit //= 2
     grad_rows = grad_rows[0]
-    key_grad = key_part[0]
-    for got in got_keys:
-        key_grad = key_grad + got.astype(jnp.float32)
     return (
         grad_rows[:lines].reshape(own_rows, index_heads, index_width),
         grad_rows[lines:].reshape(own_rows, index_heads),

time: 52.1 us -> 51.2 us (0.983)
  starting transfers between devices: 19 us -> 15.7 us
  waiting for transfers between devices: 17.9 us -> 15.6 us
  local copies, waits for them, and re-layouts: 5.29 us -> 7.39 us
  Pallas kernels: 0 us -> 1.62 us
  other arithmetic: 5 us -> 6 us
    ppermute x19 -> x18, starting transfers between devices: 19 us -> 15.7 us  [swap(): return lax.ppermute(array, 'ctx', [(i, i ^ mask) for i in range(count)])]
    dot_general x2 -> x1, matrix products: 2.9 us -> 0.31 us  [dot_rows(): lax.dot_general(left, right, (((1,), (1,)), ((), ())), preferred_element_...]
    dot_general x0 -> x1, matrix products: none -> 2.52 us  [body(): jnp.dot(main_flat, latent_all, preferred_element_type=jnp.float32)]
    ppermute x19 -> x18, waiting for transfers between devices: 17.9 us -> 15.6 us  [swap(): return lax.ppermute(array, 'ctx', [(i, i ^ mask) for i in range(count)])]
    pallas_call x0 -> x1, Pallas kernels: none -> 1.62 us  [pack_keys(): pl.pallas_call(pack_kernel, out_shape=jax.ShapeDtypeStruct((lines, codes....]
    slice x3 -> x11, local copies, waits for them, and re-layouts: 1.64 us -> 3.06 us  [the longest x4 2.27 us: body(): latent_all = jnp.concatenate([b[:latent_width] for b in key_blocks], axis=1)]
    reduce_sum x1, other arithmetic: 0.59 us -> 1.29 us  [body(): target = jnp.sum(main_exp / main_total[:, :, None], axis=1) / head_count]
    exp2 x1 -> x0, other arithmetic: 0.69 us -> none  [dequantize(): factors = jnp.exp2(key_scales.astype(jnp.float32))]
  transfers between devices with their start and end apart: 19 -> 18, of which waited for: 7 -> 8; matrix products, arithmetic and copies ran while one was open for 10% -> 16% of each run, Pallas kernels for 0% -> 0%
where the time goes in v2:
time: 51.2 us; the launch traced here: 50.8 us
  starting transfers between devices  15.7 us (31%)
  waiting for transfers between devices  15.6 us (30%)
  local copies, waits for them, and re-layouts  7.39 us (14%)
  other arithmetic  6 us (12%)
  matrix products  3.58 us (7%)
  Pallas kernels  1.62 us (3%)
  between operations  0.93 us (2%)
    ppermute x18, starting transfers between devices, swap(): return lax.ppermute(array, 'ctx', [(i, i ^ mask) for i in range(count)])  15.7 us
    ppermute x18, waiting for transfers between devices, swap(): return lax.ppermute(array, 'ctx', [(i, i ^ mask) for i in range(count)])  15.6 us
    dot_general x1, matrix products, body(): jnp.dot(main_flat, latent_all, preferred_element_type=jnp.float32)  2.52 us
    slice x4, local copies, waits for them, and re-layouts, body(): latent_all = jnp.concatenate([b[:latent_width] for b in key_blocks], axis=1)  2.27 us
    unnamed x21, local copies, waits for them, and re-layouts  1.88 us
    pallas_call x1, Pallas kernels, pack_keys(): pl.pallas_call(pack_kernel, out_shape=jax.ShapeDtypeStruct((lines, codes....  1.62 us
    reduce_sum x1, other arithmetic, body(): target = jnp.sum(main_exp / main_total[:, :, None], axis=1) / head_count  1.29 us
  transfers between devices with their start and end apart: 18, of which 8 were waited for; matrix products, arithmetic and copies ran while one was open for 16% of the time, Pallas kernels for 0%

profile of v2, /device:TPU:0, one launch (start us, length us, event | category | flops | bytes accessed | tf_op | source)
XLA Modules:
  0.0 50.8 jit_solution(3267924765044375371)
XLA Ops:
  0.6 1.6 %pack_keys.1 = bf16[704,128]{1,0:T(8,128)(2,1)} custom-call(bf16[576,128]{1,0:T(8,128)(2,1)} %bitcast.37, s32[4,128]{1,0:T(4,128)} %bitcast.46, bf16[128,128]{1,0:T(8,128)(2,1)} %keys_ref.1), custom_call_target="tpu_custom_call" | custom-call | tf_op jit(solution)/shard_map/pack_keys/pallas_call | solution.py:35
  2.3 0.7 %convert_bitcast_fusion = f32[2,1]{0,1:T(1,128)S(1)} fusion(s32[2]{0:T(128)} %param.13), kind=kLoop, calls=%fused_computation.62 | loop fusion | flops 2 | bytes 16 | tf_op jit(solution)/shard_map/broadcast_in_dim | solution.py:73
  2.9 0.1 copy.15
  3.0 0.8 %pad_maximum_fusion.5 = f32[2,65]{1,0:T(2,128)S(1)} fusion(f32[2,1]{1,0:T(2,128)S(1)} %copy.15, f32[2,64]{1,0:T(2,128)} %param.12), kind=kLoop, calls=%fused_computation.59 | loop fusion | flops 130 | bytes 1040 | tf_op jit(solution)/shard_map/concatenate | solution.py:73
  3.8 3.0 %collective-permute-start.7 = (f32[2,65]{1,0:T(2,128)S(1)}, f32[2,65]{1,0:T(2,128)S(1)}, u32[]{:S(2)}, u32[]{:S(2)}) collective-permute-start(f32[2,65]{1,0:T(2,128)S(1)} %pad_maximum_fusion.5), channel_id=1, source_target_pairs={{0,2},{1,3},{2,0},{3,1},{4,6},{5,7},{6,4},{7,5},{8,10},{9,11},{10,... | collective-permute-start | bytes 1568 | tf_op jit(solution)/shard_map/ppermute | solution.py:43
  6.7 0.1 collective-permute-start.1
  6.8 0.4 collective-permute-start
  7.2 2.8 %collective-permute-start.4 = (bf16[704,128]{1,0:T(8,128)(2,1)}, bf16[704,128]{1,0:T(8,128)(2,1)S(1)}, u32[]{:S(2)}, u32[]{:S(2)}) collective-permute-start(bf16[704,128]{1,0:T(8,128)(2,1)} %pack_keys.1), channel_id=1, source_target_pairs={{0,8},{1,9},{2,10},{3,11},{4,12},{5,13},{6,14},{7,15},{8,0},{9,1},... | collective-permute-start | bytes 540680 | tf_op jit(solution)/shard_map/ppermute | solution.py:43
  10.3 0.8 %constant_dynamic-update-slice_fusion.3 = bf16[8,64,128]{2,1,0:T(8,128)(2,1)S(1)} fusion(bf16[2,64,128]{2,1,0:T(8,128)(2,1)} %param.11), kind=kLoop, calls=%fused_computation.45 | loop fusion | bytes 65536
  11.0 0.8 %slice.96 = bf16[128,128]{1,0:T(8,128)(2,1)S(1)} slice(bf16[704,128]{1,0:T(8,128)(2,1)} %pack_keys.1), slice={[576:704], [0:128]} | slice | bytes 65536 | tf_op jit(solution)/shard_map/slice | solution.py:79
  11.8 0.9 %slice.102 = bf16[576,128]{1,0:T(8,128)(2,1)S(1)} slice(bf16[704,128]{1,0:T(8,128)(2,1)} %pack_keys.1), slice={[0:576], [0:128]} | slice | bytes 294912 | tf_op jit(solution)/shard_map/slice | solution.py:78
  12.7 1.6 %collective-permute-start.3 = (bf16[704,128]{1,0:T(8,128)(2,1)}, bf16[704,128]{1,0:T(8,128)(2,1)S(1)}, u32[]{:S(2)}, u32[]{:S(2)}) collective-permute-start(bf16[704,128]{1,0:T(8,128)(2,1)} %pack_keys.1), channel_id=1, source_target_pairs={{0,4},{1,5},{2,6},{3,7},{4,0},{5,1},{6,2},{7,3},{8,12},{9,13},{10,... | collective-permute-start | bytes 540680 | tf_op jit(solution)/shard_map/ppermute | solution.py:43
  14.4 1.5 %collective-permute-start.10 = (bf16[2,128,576]{1,2,0:T(8,128)(2,1)}, bf16[2,128,576]{1,2,0:T(8,128)(2,1)S(1)}, u32[]{:S(2)}, u32[]{:S(2)}) collective-permute-start(bf16[2,128,576]{1,2,0:T(8,128)(2,1)} %param.7), channel_id=1, source_target_pairs={{0,2},{1,3},{2,0},{3,1},{4,6},{5,7},{6,4},{7,5},{8,10},{9,11},{10,... | collective-permute-start | bytes 884744 | tf_op jit(solution)/shard_map/ppermute | solution.py:43
  15.8 0.8 %pad_maximum_fusion.4 = f32[8,65]{1,0:T(8,128)S(1)} fusion(f32[2,65]{1,0:T(2,128)S(1)} %collective-permute-done.8, f32[2,65]{1,0:T(2,128)S(1)} %collective-permute-done.7, f32[2,65]{1,0:T(2,128)S(1)} %collective-permute-done.6, f32[2,1]{1,0:T(2,128)S(1)} %copy.15, f32[2,64]{1,0:T(2,128)} %param.12), kind=kLoop, calls=%fused_computation.55 | loop fusion | flops 2080 | bytes 4160 | tf_op jit(solution)/shard_map/concatenate | solution.py:82
  16.6 0.2 convert_reduce_fusion
  16.8 0.7 %broadcast_compare_fusion = pred[8,512]{1,0:T(8,128)(4,1)} fusion(s32[512]{0:T(512)S(1)} %add_bitcast_fusion, s32[8]{0:T(128)S(1)} %convert_reduce_fusion), kind=kLoop, calls=%fused_computation.53 | loop fusion | flops 4096 | bytes 6176 | tf_op jit(solution)/shard_map/le | solution.py:87
  17.5 0.5 collective-permute-start.2
  18.0 1.3 %collective-permute-done.4 = bf16[704,128]{1,0:T(8,128)(2,1)S(1)} collective-permute-done((bf16[704,128]{1,0:T(8,128)(2,1)}, bf16[704,128]{1,0:T(8,128)(2,1)S(1)}, u32[]{:S(2)}, u32[]{:S(2)}) %collective-permute-start.4) | collective-permute-done | bytes 180256 | tf_op jit(solution)/shard_map/ppermute | solution.py:43
  19.3 0.8 %collective-permute-start.5 = (bf16[704,128]{1,0:T(8,128)(2,1)S(1)}, bf16[704,128]{1,0:T(8,128)(2,1)S(1)}, u32[]{:S(2)}, u32[]{:S(2)}) collective-permute-start(bf16[704,128]{1,0:T(8,128)(2,1)S(1)} %collective-permute-done.4), channel_id=1, source_target_pairs={{0,4},{1,5},{2,6},{3,7},{4,0},{5,1},{6,2},{7,3},{8,12},{9,13},{10,... | collective-permute-start | bytes 540680 | tf_op jit(solution)/shard_map/ppermute | solution.py:43
  20.1 0.7 %slice.129 = bf16[576,128]{1,0:T(8,128)(2,1)} slice(bf16[704,128]{1,0:T(8,128)(2,1)S(1)} %collective-permute-done.4), slice={[0:576], [0:128]} | slice | bytes 294912 | tf_op jit(solution)/shard_map/slice | solution.py:78
  20.7 2.4 %collective-permute-done.3 = bf16[704,128]{1,0:T(8,128)(2,1)S(1)} collective-permute-done((bf16[704,128]{1,0:T(8,128)(2,1)}, bf16[704,128]{1,0:T(8,128)(2,1)S(1)}, u32[]{:S(2)}, u32[]{:S(2)}) %collective-permute-start.3) | collective-permute-done | bytes 180256 | tf_op jit(solution)/shard_map/ppermute | solution.py:43
  23.1 0.7 %slice.128 = bf16[576,128]{1,0:T(8,128)(2,1)} slice(bf16[704,128]{1,0:T(8,128)(2,1)S(1)} %collective-permute-done.3), slice={[0:576], [0:128]} | slice | bytes 294912 | tf_op jit(solution)/shard_map/slice | solution.py:78
  23.8 2.7 %collective-permute-done.5 = bf16[704,128]{1,0:T(8,128)(2,1)S(1)} collective-permute-done((bf16[704,128]{1,0:T(8,128)(2,1)S(1)}, bf16[704,128]{1,0:T(8,128)(2,1)S(1)}, u32[]{:S(2)}, u32[]{:S(2)}) %collective-permute-start.5) | collective-permute-done | bytes 180256 | tf_op jit(solution)/shard_map/ppermute | solution.py:43
  26.5 0.3 multiply_reduce_fusion.1
  26.8 0.2 fusion.21
  27.0 0.1 concatenate.50
  27.2 0.4 copy-done.6
  27.5 0.7 %copy-done.8 = bf16[2,128,576]{1,2,0:T(8,128)(2,1)} copy-done((bf16[2,128,576]{1,2,0:T(8,128)(2,1)}, bf16[2,128,576]{1,2,0:T(8,128)(2,1)S(1)}, u32[]{:S(2)}) %copy-start.8) | copy-done | bytes 294936
  28.2 2.5 %fusion = (f32[8,128]{1,0:T(8,128)S(1)}, f32[8,128,512]{2,1,0:T(8,128)S(1)}) fusion(pred[8,512]{1,0:T(8,128)(4,1)} %broadcast_compare_fusion, bf16[576,128]{1,0:T(8,128)(2,1)S(1)} %slice.130, bf16[576,128]{1,0:T(8,128)(2,1)} %slice.129, bf16[576,128]{1,0:T(8,128)(2,1)} %slice.128, bf16[576,128]{1,0:T(8,128)(2,1)S(1)} %slice.102, ...), kind=kOutput, calls=%fused_computation.2 | convolution fusion | flops 609680384 | bytes 3874816 | tf_op jit(solution)/shard_map/dot_general | solution.py:89
  30.8 1.6 %collective-permute-start.12 = (f32[4,2,129]{2,1,0:T(2,128)S(1)}, f32[4,2,129]{2,1,0:T(2,128)S(1)}, u32[]{:S(2)}, u32[]{:S(2)}) collective-permute-start(f32[4,2,129]{2,1,0:T(2,128)S(1)} %pad_maximum_fusion.1), channel_id=1, source_target_pairs={{0,2},{1,3},{2,0},{3,1},{4,6},{5,7},{6,4},{7,5},{8,10},{9,11},{10,... | collective-permute-start | bytes 12392 | tf_op jit(solution)/shard_map/ppermute | solution.py:43
  32.4 2.1 %collective-permute-done.12 = f32[4,2,129]{2,1,0:T(2,128)S(1)} collective-permute-done((f32[4,2,129]{2,1,0:T(2,128)S(1)}, f32[4,2,129]{2,1,0:T(2,128)S(1)}, u32[]{:S(2)}, u32[]{:S(2)}) %collective-permute-start.12) | collective-permute-done | bytes 4160 | tf_op jit(solution)/shard_map/ppermute | solution.py:43
  34.6 0.1 fusion.15
  34.7 0.7 %copy.16 = f32[8,1]{1,0:T(8,128)S(1)} copy(f32[8,1]{0,1:T(1,128)} %bitcast.45) | data formatting | bytes 64 | tf_op jit(solution)/shard_map/concatenate | solution.py:95
  35.5 0.3 collective-permute-done.13
  35.8 0.1 slice_reduce_fusion
  35.9 1.3 %divide_reduce_fusion = f32[8,512]{1,0:T(8,128)S(1)} fusion(f32[8,128,512]{2,1,0:T(8,128)S(1)} %get-tuple-element.26, f32[8,128]{1,0:T(8,128)S(1)} %slice.138, pred[8,512]{1,0:T(8,128)(4,1)} %broadcast_compare_fusion), kind=kLoop, calls=%fused_computation.1 | loop fusion | flops 2093056 | bytes 2121728 | tf_op jit(solution)/shard_map/reduce_sum | solution.py:107
  37.3 0.5 convolution_bitcast_fusion
  37.8 0.2 select_convert_fusion
  38.1 0.2 multiply_reduce_fusion
  38.3 1.6 %collective-permute-start.16 = (bf16[2,128,128]{2,1,0:T(8,128)(2,1)S(1)}, bf16[2,128,128]{2,1,0:T(8,128)(2,1)S(1)}, u32[]{:S(2)}, u32[]{:S(2)}) collective-permute-start(bf16[2,128,128]{2,1,0:T(8,128)(2,1)S(1)} %bitcast.41), channel_id=1, source_target_pairs={{0,8},{1,9},{2,10},{3,11},{4,12},{5,13},{6,14},{7,15},{8,0},{9,1},... | collective-permute-start | bytes 196616 | tf_op jit(solution)/shard_map/ppermute | solution.py:43
  39.9 0.3 fusion.19
  40.2 1.6 %collective-permute-start.14 = (f32[2,129,128]{2,1,0:T(8,128)S(1)}, f32[2,129,128]{2,1,0:T(8,128)S(1)}, u32[]{:S(2)}, u32[]{:S(2)}) collective-permute-start(f32[2,129,128]{2,1,0:T(8,128)S(1)} %pad_maximum_fusion), channel_id=1, source_target_pairs={{0,2},{1,3},{2,0},{3,1},{4,6},{5,7},{6,4},{7,5},{8,10},{9,11},{10,... | collective-permute-start | bytes 396296 | tf_op jit(solution)/shard_map/ppermute | solution.py:43
  41.8 3.1 %collective-permute-done.16 = bf16[2,128,128]{2,1,0:T(8,128)(2,1)S(1)} collective-permute-done((bf16[2,128,128]{2,1,0:T(8,128)(2,1)S(1)}, bf16[2,128,128]{2,1,0:T(8,128)(2,1)S(1)}, u32[]{:S(2)}, u32[]{:S(2)}) %collective-permute-start.16) | collective-permute-done | bytes 65568 | tf_op jit(solution)/shard_map/ppermute | solution.py:43
  45.0 0.8 %collective-permute-done.14 = f32[2,129,128]{2,1,0:T(8,128)S(1)} collective-permute-done((f32[2,129,128]{2,1,0:T(8,128)S(1)}, f32[2,129,128]{2,1,0:T(8,128)S(1)}, u32[]{:S(2)}, u32[]{:S(2)}) %collective-permute-start.14) | collective-permute-done | bytes 132128 | tf_op jit(solution)/shard_map/ppermute | solution.py:43
  45.9 2.9 %collective-permute-done.17 = bf16[1,128,128]{2,1,0:T(8,128)(2,1)S(1)} collective-permute-done((bf16[1,128,128]{2,1,0:T(8,128)(2,1)S(1)}, bf16[1,128,128]{2,1,0:T(8,128)(2,1)S(1)}, u32[]{:S(2)}, u32[]{:S(2)}) %collective-permute-start.17) | collective-permute-done | bytes 32800 | tf_op jit(solution)/shard_map/ppermute | solution.py:43
  48.9 0.6 %fusion.18 = f32[128,128]{1,0:T(8,128)} fusion(f32[2,128,128]{2,1,0:T(8,128)S(1)} %convert_add_fusion, bf16[1,128,128]{2,1,0:T(8,128)(2,1)S(1)} %collective-permute-done.17), kind=kLoop, calls=%fused_computation.36 | loop fusion | flops 32768 | bytes 163840 | tf_op jit(solution)/shard_map/squeeze | solution.py:127
  49.6 0.6 %slice.143 = f32[1,128,128]{2,1,0:T(8,128)} slice(f32[1,129,128]{2,1,0:T(8,128)S(1)} %slice_add_fusion), slice={[0:1], [0:128], [0:128]} | slice | bytes 131072 | tf_op jit(solution)/shard_map/slice | solution.py:143
  50.2 0.6 %reshape.218 = f32[2,64]{1,0:T(2,128)} reshape(f32[128]{0:T(128)S(1)} %slice_reduce_fusion.1) | data formatting | bytes 1024 | tf_op jit(solution)/shard_map/reshape | solution.py:144
  (64 shorter events, 0.8 us)
Async XLA Ops:
  3.8 6.5 %collective-permute-start.7 = (f32[2,65]{1,0:T(2,128)S(1)}, f32[2,65]{1,0:T(2,128)S(1)}, u32[]{:S(2)}, u32[]{:S(2)}) collective-permute-start(f32[2,65]{1,0:T(2,128)S(1)} %pad_maximum_fusion.5), channel_id=1, source_target_pairs={{0,2},{1,3},{2,0},{3,1},{4,6},{5,7},{6,4},{7,5},{8,10},{9,11},{10,... | collective-permute-start | bytes 1568 | tf_op jit(solution)/shard_map/ppermute | solution.py:43
  6.7 6.0 %collective-permute-start.6 = (f32[2,65]{1,0:T(2,128)S(1)}, f32[2,65]{1,0:T(2,128)S(1)}, u32[]{:S(2)}, u32[]{:S(2)}) collective-permute-start(f32[2,65]{1,0:T(2,128)S(1)} %pad_maximum_fusion.5), channel_id=1, source_target_pairs={{0,1},{1,0},{2,3},{3,2},{4,5},{5,4},{6,7},{7,6},{8,9},{9,8},{10,11... | collective-permute-start | bytes 1568 | tf_op jit(solution)/shard_map/ppermute | solution.py:43
  6.7 10.7 %collective-permute-start.1 = (bf16[2,64,128]{2,1,0:T(8,128)(2,1)}, bf16[2,64,128]{2,1,0:T(8,128)(2,1)S(1)}, u32[]{:S(2)}, u32[]{:S(2)}) collective-permute-start(bf16[2,64,128]{2,1,0:T(8,128)(2,1)} %param.11), channel_id=1, source_target_pairs={{0,2},{1,3},{2,0},{3,1},{4,6},{5,7},{6,4},{7,5},{8,10},{9,11},{10,... | collective-permute-start | bytes 98312 | tf_op jit(solution)/shard_map/ppermute | solution.py:43
  6.8 10.7 %collective-permute-start = (bf16[2,64,128]{2,1,0:T(8,128)(2,1)}, bf16[2,64,128]{2,1,0:T(8,128)(2,1)S(1)}, u32[]{:S(2)}, u32[]{:S(2)}) collective-permute-start(bf16[2,64,128]{2,1,0:T(8,128)(2,1)} %param.11), channel_id=1, source_target_pairs={{0,1},{1,0},{2,3},{3,2},{4,5},{5,4},{6,7},{7,6},{8,9},{9,8},{10,11... | collective-permute-start | bytes 98312 | tf_op jit(solution)/shard_map/ppermute | solution.py:43
  7.2 12.0 %collective-permute-start.4 = (bf16[704,128]{1,0:T(8,128)(2,1)}, bf16[704,128]{1,0:T(8,128)(2,1)S(1)}, u32[]{:S(2)}, u32[]{:S(2)}) collective-permute-start(bf16[704,128]{1,0:T(8,128)(2,1)} %pack_keys.1), channel_id=1, source_target_pairs={{0,8},{1,9},{2,10},{3,11},{4,12},{5,13},{6,14},{7,15},{8,0},{9,1},... | collective-permute-start | bytes 540680 | tf_op jit(solution)/shard_map/ppermute | solution.py:43
  10.2 4.1 %collective-permute-start.8 = (f32[2,65]{1,0:T(2,128)S(1)}, f32[2,65]{1,0:T(2,128)S(1)}, u32[]{:S(2)}, u32[]{:S(2)}) collective-permute-start(f32[2,65]{1,0:T(2,128)S(1)} %collective-permute-done.7), channel_id=1, source_target_pairs={{0,1},{1,0},{2,3},{3,2},{4,5},{5,4},{6,7},{7,6},{8,9},{9,8},{10,11... | collective-permute-start | bytes 1568 | tf_op jit(solution)/shard_map/ppermute | solution.py:43
  12.7 10.4 %collective-permute-start.3 = (bf16[704,128]{1,0:T(8,128)(2,1)}, bf16[704,128]{1,0:T(8,128)(2,1)S(1)}, u32[]{:S(2)}, u32[]{:S(2)}) collective-permute-start(bf16[704,128]{1,0:T(8,128)(2,1)} %pack_keys.1), channel_id=1, source_target_pairs={{0,4},{1,5},{2,6},{3,7},{4,0},{5,1},{6,2},{7,3},{8,12},{9,13},{10,... | collective-permute-start | bytes 540680 | tf_op jit(solution)/shard_map/ppermute | solution.py:43
  14.4 9.4 %collective-permute-start.10 = (bf16[2,128,576]{1,2,0:T(8,128)(2,1)}, bf16[2,128,576]{1,2,0:T(8,128)(2,1)S(1)}, u32[]{:S(2)}, u32[]{:S(2)}) collective-permute-start(bf16[2,128,576]{1,2,0:T(8,128)(2,1)} %param.7), channel_id=1, source_target_pairs={{0,2},{1,3},{2,0},{3,1},{4,6},{5,7},{6,4},{7,5},{8,10},{9,11},{10,... | collective-permute-start | bytes 884744 | tf_op jit(solution)/shard_map/ppermute | solution.py:43
  16.8 10.3 %copy-start.4 = (s32[8]{0:T(128)}, s32[8]{0:T(128)S(1)}, u32[]{:S(2)}) copy-start(s32[8]{0:T(128)S(1)} %convert_reduce_fusion) | copy-start | bytes 100
  17.5 9.7 %collective-permute-start.9 = (bf16[2,128,576]{1,2,0:T(8,128)(2,1)}, bf16[2,128,576]{1,2,0:T(8,128)(2,1)S(1)}, u32[]{:S(2)}, u32[]{:S(2)}) collective-permute-start(bf16[2,128,576]{1,2,0:T(8,128)(2,1)} %param.7), channel_id=1, source_target_pairs={{0,1},{1,0},{2,3},{3,2},{4,5},{5,4},{6,7},{7,6},{8,9},{9,8},{10,11... | collective-permute-start | bytes 884744 | tf_op jit(solution)/shard_map/ppermute | solution.py:43
  17.5 2.6 %collective-permute-start.2 = (bf16[2,64,128]{2,1,0:T(8,128)(2,1)S(1)}, bf16[2,64,128]{2,1,0:T(8,128)(2,1)S(1)}, u32[]{:S(2)}, u32[]{:S(2)}) collective-permute-start(bf16[2,64,128]{2,1,0:T(8,128)(2,1)S(1)} %collective-permute-done.1), channel_id=1, source_target_pairs={{0,1},{1,0},{2,3},{3,2},{4,5},{5,4},{6,7},{7,6},{8,9},{9,8},{10,11... | collective-permute-start | bytes 98312 | tf_op jit(solution)/shard_map/ppermute | solution.py:43
  19.3 7.2 %collective-permute-start.5 = (bf16[704,128]{1,0:T(8,128)(2,1)S(1)}, bf16[704,128]{1,0:T(8,128)(2,1)S(1)}, u32[]{:S(2)}, u32[]{:S(2)}) collective-permute-start(bf16[704,128]{1,0:T(8,128)(2,1)S(1)} %collective-permute-done.4), channel_id=1, source_target_pairs={{0,4},{1,5},{2,6},{3,7},{4,0},{5,1},{6,2},{7,3},{8,12},{9,13},{10,... | collective-permute-start | bytes 540680 | tf_op jit(solution)/shard_map/ppermute | solution.py:43
  23.1 7.7 %copy-start = (bf16[128,128]{1,0:T(8,128)(2,1)}, bf16[128,128]{1,0:T(8,128)(2,1)S(1)}, u32[]{:S(2)}) copy-start(bf16[128,128]{1,0:T(8,128)(2,1)S(1)} %slice.125) | copy-start | bytes 98308
  23.8 3.4 %copy-start.7 = (bf16[2,128,576]{1,2,0:T(8,128)(2,1)}, bf16[2,128,576]{1,2,0:T(8,128)(2,1)S(1)}, u32[]{:S(2)}) copy-start(bf16[2,128,576]{1,2,0:T(8,128)(2,1)S(1)} %collective-permute-done.10) | copy-start | bytes 884740
  23.8 4.5 %collective-permute-start.11 = (bf16[2,128,576]{1,2,0:T(8,128)(2,1)S(1)}, bf16[2,128,576]{1,2,0:T(8,128)(2,1)}, u32[]{:S(2)}, u32[]{:S(2)}) collective-permute-start(bf16[2,128,576]{1,2,0:T(8,128)(2,1)S(1)} %collective-permute-done.10), channel_id=1, source_target_pairs={{0,1},{1,0},{2,3},{3,2},{4,5},{5,4},{6,7},{7,6},{8,9},{9,8},{10,11... | collective-permute-start | bytes 884744 | tf_op jit(solution)/shard_map/ppermute | solution.py:43
  26.5 0.7 %copy-start.2 = (bf16[128,128]{1,0:T(8,128)(2,1)}, bf16[128,128]{1,0:T(8,128)(2,1)S(1)}, u32[]{:S(2)}) copy-start(bf16[128,128]{1,0:T(8,128)(2,1)S(1)} %slice.127) | copy-start | bytes 98308
  27.0 0.5 %copy-start.6 = (f32[8]{0:T(128)}, f32[8]{0:T(128)S(1)}, u32[]{:S(2)}) copy-start(f32[8]{0:T(128)S(1)} %fusion.21) | copy-start | bytes 100
  27.5 0.7 %copy-start.8 = (bf16[2,128,576]{1,2,0:T(8,128)(2,1)}, bf16[2,128,576]{1,2,0:T(8,128)(2,1)S(1)}, u32[]{:S(2)}) copy-start(bf16[2,128,576]{1,2,0:T(8,128)(2,1)S(1)} %collective-permute-done.9) | copy-start | bytes 884740
  30.8 6.5 %copy-start.5 = (s32[8]{0:T(128)S(1)}, s32[8]{0:T(128)}, u32[]{:S(2)}) copy-start(s32[8]{0:T(128)} %copy-done.4) | copy-start | bytes 100
  30.8 3.7 %collective-permute-start.12 = (f32[4,2,129]{2,1,0:T(2,128)S(1)}, f32[4,2,129]{2,1,0:T(2,128)S(1)}, u32[]{:S(2)}, u32[]{:S(2)}) collective-permute-start(f32[4,2,129]{2,1,0:T(2,128)S(1)} %pad_maximum_fusion.1), channel_id=1, source_target_pairs={{0,2},{1,3},{2,0},{3,1},{4,6},{5,7},{6,4},{7,5},{8,10},{9,11},{10,... | collective-permute-start | bytes 12392 | tf_op jit(solution)/shard_map/ppermute | solution.py:43
  34.5 1.2 %collective-permute-start.13 = (f32[4,2,129]{2,1,0:T(2,128)S(1)}, f32[4,2,129]{2,1,0:T(2,128)S(1)}, u32[]{:S(2)}, u32[]{:S(2)}) collective-permute-start(f32[4,2,129]{2,1,0:T(2,128)S(1)} %get-tuple-element.16), channel_id=1, source_target_pairs={{0,1},{1,0},{2,3},{3,2},{4,5},{5,4},{6,7},{7,6},{8,9},{9,8},{10,11... | collective-permute-start | bytes 12392 | tf_op jit(solution)/shard_map/ppermute | solution.py:43
  37.3 2.6 %copy-start.1 = (bf16[128,128]{1,0:T(8,128)(2,1)S(1)}, bf16[128,128]{1,0:T(8,128)(2,1)}, u32[]{:S(2)}) copy-start(bf16[128,128]{1,0:T(8,128)(2,1)} %copy-done) | copy-start | bytes 98308
  37.3 2.6 %copy-start.3 = (bf16[128,128]{1,0:T(8,128)(2,1)S(1)}, bf16[128,128]{1,0:T(8,128)(2,1)}, u32[]{:S(2)}) copy-start(bf16[128,128]{1,0:T(8,128)(2,1)} %copy-done.2) | copy-start | bytes 98308
  38.3 6.5 %collective-permute-start.16 = (bf16[2,128,128]{2,1,0:T(8,128)(2,1)S(1)}, bf16[2,128,128]{2,1,0:T(8,128)(2,1)S(1)}, u32[]{:S(2)}, u32[]{:S(2)}) collective-permute-start(bf16[2,128,128]{2,1,0:T(8,128)(2,1)S(1)} %bitcast.41), channel_id=1, source_target_pairs={{0,8},{1,9},{2,10},{3,11},{4,12},{5,13},{6,14},{7,15},{8,0},{9,1},... | collective-permute-start | bytes 196616 | tf_op jit(solution)/shard_map/ppermute | solution.py:43
  40.2 5.6 %collective-permute-start.14 = (f32[2,129,128]{2,1,0:T(8,128)S(1)}, f32[2,129,128]{2,1,0:T(8,128)S(1)}, u32[]{:S(2)}, u32[]{:S(2)}) collective-permute-start(f32[2,129,128]{2,1,0:T(8,128)S(1)} %pad_maximum_fusion), channel_id=1, source_target_pairs={{0,2},{1,3},{2,0},{3,1},{4,6},{5,7},{6,4},{7,5},{8,10},{9,11},{10,... | collective-permute-start | bytes 396296 | tf_op jit(solution)/shard_map/ppermute | solution.py:43
  44.9 4.0 %collective-permute-start.17 = (bf16[1,128,128]{2,1,0:T(8,128)(2,1)S(1)}, bf16[1,128,128]{2,1,0:T(8,128)(2,1)S(1)}, u32[]{:S(2)}, u32[]{:S(2)}) collective-permute-start(bf16[1,128,128]{2,1,0:T(8,128)(2,1)S(1)} %slice.167), channel_id=1, source_target_pairs={{0,4},{1,5},{2,6},{3,7},{4,0},{5,1},{6,2},{7,3},{8,12},{9,13},{10,... | collective-permute-start | bytes 98312 | tf_op jit(solution)/shard_map/ppermute | solution.py:43
  45.9 3.7 %collective-permute-start.15 = (f32[1,129,128]{2,1,0:T(8,128)S(1)}, f32[1,129,128]{2,1,0:T(8,128)S(1)}, u32[]{:S(2)}, u32[]{:S(2)}) collective-permute-start(f32[1,129,128]{2,1,0:T(8,128)S(1)} %slice.142), channel_id=1, source_target_pairs={{0,1},{1,0},{2,3},{3,2},{4,5},{5,4},{6,7},{7,6},{8,9},{9,8},{10,11... | collective-permute-start | bytes 198152 | tf_op jit(solution)/shard_map/ppermute | solution.py:43
